TPU v7x, 32 devices: a whole 2x2x4 slice. The times are simulated.
32 devices in a mesh: row: 4 (over y, core), col: 8 (over z, x).
Axes of the slice: x: 2, y: 2, z: 4, core: 2. Of those that a mesh axis runs over, the one named last changes fastest.
Arguments:
- user_factors: float32 [8192, 128], P('row'), may hold values from -6 to 6
- item_factors: float32 [32768, 128], P(('row', 'col')), may hold values from -0.03125 to 0.03125
- fetch_list: int32 [4, 8, 32, 1], P('row', 'col'), may hold values from 0 to 7
- tile_user: int32 [4, 8, 32], P('row', 'col'), may hold values from 0 to 15
- tile_slot: int32 [4, 8, 32], P('row', 'col'), may hold values from 0 to 31
- entry_row: int32 [4, 8, 32, 512], P('row', 'col'), may hold values from 0 to 127
- entry_col: int32 [4, 8, 32, 512], P('row', 'col'), may hold values from 0 to 127
- entry_count: int32 [4, 8, 32, 512], P('row', 'col'), may hold values from 1 to 8
- tile_count: int32 [4, 8], P('row', 'col'), may hold values from 4 to 32, as said below
Outputs:
- solved: float32 [8192, 128], P('row')
Inputs may be any that keep to these rules, and one draw needn't show every extreme that they name: `tile_count`: at least 4 tiles live on every device; some device has all 32 live in every draw.
All inputs are finite; a program needn't handle non-finite values.
Results may differ from a plain program's by a relative error of at most 0.0003.
Values sent between devices are 32-bit elements; how exact they have to be, the bound alone decides.
No kernel may reach another device: no remote copies, remote signals or barrier semaphores. Data moves between devices by JAX's collectives and lax.ppermute only.
A program may use at most 128 MiB of HBM per device.

v0:
```python
import jax
import jax.numpy as jnp
from jax import lax
from jax.experimental import pallas as pl
from jax.experimental.pallas import tpu as pltpu
from jax.sharding import PartitionSpec as P


K = 128
BLOCK = 128
ITERS = 3
CONFIDENCE_SCALE = 40.0
RIDGE = 0.5
EPSILON = 1e-06
GROUP_BITS = 3
GROUP = 1 << GROUP_BITS
RADIX = 1024.0
F32 = jnp.float32
BF16 = jnp.bfloat16
NT = (((1,), (1,)), ((), ()))
NN = (((1,), (0,)), ((), ()))


def halves(value):
    high = value.astype(BF16)
    return high, (value - high.astype(F32)).astype(BF16)


def dot(a, b, dims):
    return lax.dot_general(a, b, dims, preferred_element_type=F32)


def dot3(a, b_high, b_low):
    a_high, a_low = halves(a)
    return dot(a_high, b_high, NN) + dot(a_high, b_low, NN) + dot(a_low, b_high, NN)


def pair_scores(v_high, v_low, y_both):
    wide = dot(v_high, y_both, NT)
    return wide[:, :BLOCK] + wide[:, BLOCK:] + dot(v_low, y_both[:BLOCK], NT)


def pair_pull(weights, y_both):
    high, low = halves(weights)
    return dot(jnp.concatenate([high, high], axis=1), y_both, NN) + dot(low, y_both[:BLOCK], NN)


def decode(code):
    counts = jnp.floor(code * (1.0 / RADIX))
    return counts * CONFIDENCE_SCALE, code - counts * RADIX


def row_dot(a, b):
    high, low = halves(a * b)
    return dot(jnp.concatenate([high, low], axis=1), jnp.ones((2 * K, K), BF16), NN)


def row_sums(value):
    high, low = halves(value)
    return dot(jnp.ones((8, 2 * K), BF16), jnp.concatenate([high, low], axis=1), NT)[:1]


def build_kernel(tiles, part_blocks, owned, sides, mine_ref, *rest):
    sources = len(rest) - 9
    given = rest[:sources]
    list_ref, total_ref, dense_ref, index, facts, entry_ref, buf, sem, sem_e = rest[sources:]
    rows = given[0].shape[0]
    fact_copies = [
        pltpu.make_async_copy(ref.at[pl.ds(3 * tiles, 8), pl.ds(0, BLOCK)], facts.at[s], sem_e.at[0, s])
        for s, ref in enumerate(given)
    ]
    entry_copies = [
        pltpu.make_async_copy(ref, entry_ref.at[pl.ds(s * rows, rows)], sem_e.at[1, s])
        for s, ref in enumerate(given)
    ]
    for copy in fact_copies + entry_copies:
        copy.start()
    for copy in fact_copies:
        copy.wait()
    my_z, my_x, flip = mine_ref[0], mine_ref[1], mine_ref[2]
    owned_bits, part_bits = owned.bit_length() - 1, part_blocks.bit_length() - 1
    side_blocks = part_blocks // sides
    side_bits = side_blocks.bit_length() - 1
    last = list_ref.shape[0] // GROUP - 1

    def spot(k, side):
        back = ((last - (k >> GROUP_BITS)) << GROUP_BITS) | (k & (GROUP - 1))
        return jnp.where(side == 1, back, k)

    totals = (jnp.int32(0), jnp.int32(0))
    for source in range(sources):

        def scan(t, n, source=source):
            user = facts[source, 0, t]
            item = facts[source, 1, t]
            side = (user >> side_bits) & (sides - 1)
            at = spot(jnp.where(side == 1, n[1], n[0]), side)
            index[at] = source * rows + t
            list_ref[at] = ((user & (side_blocks - 1)) << 16) | ((item & (owned - 1)) ^ flip)
            missed = ((item >> owned_bits) ^ my_x) | ((user >> part_bits) ^ my_z)
            hit = jnp.where(missed == 0, 1, 0).astype(jnp.int32)
            return n[0] + hit * (1 - side), n[1] + hit * side

        totals = lax.fori_loop(0, tiles, scan, totals, unroll=8)
    chunks = []
    for side in range(2):
        total_ref[side] = totals[side]
        chunks.append((totals[side] + (GROUP - 1)) >> GROUP_BITS)
        for extra in range(GROUP - 1):
            k = totals[side] + extra

            @pl.when(k < chunks[side] * GROUP)
            def _():
                at = spot(k, side)
                index[at] = 0
                list_ref[at] = 0

    for copy in entry_copies:
        copy.wait()
    ids = lax.broadcasted_iota(jnp.int32, (BLOCK, entry_ref.shape[1]), 0)

    def out_copy(chunk, slot):
        return pltpu.make_async_copy(buf.at[slot], dense_ref.at[pl.ds(chunk * GROUP, GROUP)], sem.at[slot])

    def step(j, carry):
        slot = j & 1
        front = j < chunks[0]
        chunk = jnp.where(front, j, last - (j - chunks[0]))
        left = jnp.where(front, totals[0] - j * GROUP, totals[1] - (j - chunks[0]) * GROUP)

        @pl.when(j >= 2)
        def _():
            out_copy(0, slot).wait()

        for u in range(GROUP):
            base = index[chunk * GROUP + u]
            users = entry_ref[pl.ds(base, 1), :]
            items = entry_ref[pl.ds(base + tiles, 1), :]
            counts = entry_ref[pl.ds(base + 2 * tiles, 1), :].astype(F32)
            user_hot = jnp.where(ids == users, 1.0, 0.0).astype(BF16)
            hit = ids == items
            item_hot = jnp.where(hit, 1.0, 0.0).astype(BF16)
            count_hot = jnp.where(hit, counts, 0.0).astype(BF16)
            both = dot(user_hot, jnp.concatenate([item_hot, count_hot], axis=0), NT)
            live = jnp.where(u < left, 1.0, 0.0)
            buf[slot, u] = (both[:, :BLOCK] + both[:, BLOCK:] * RADIX) * live
        out_copy(chunk, slot).start()
        return carry

    every = chunks[0] + chunks[1]
    lax.fori_loop(0, every, step, 0)

    @pl.when(every >= 2)
    def _():
        out_copy(0, every & 1).wait()

    @pl.when(every >= 1)
    def _():
        out_copy(0, (every - 1) & 1).wait()


def choose(value, low, high, act):
    if high - low == 1:
        act(low)
        return
    middle = (low + high) // 2

    @pl.when(value < middle)
    def _():
        choose(value, low, middle, act)

    @pl.when(value >= middle)
    def _():
        choose(value, middle, high, act)


def start_kernel(side, owners, blocks, list_ref, total_ref, start_ref, dense_ref, *rest):
    items = rest[:owners]
    out_ref, pair_ref = rest[owners : owners + 2]
    dense, raw, both, v_high, v_low, sem_d, sem_y, sem_o = rest[owners + 2 :]
    chunks = (total_ref[side] + (GROUP - 1)) >> GROUP_BITS
    end = list_ref.shape[0] // GROUP - 1

    def place(j):
        return end - j if side else j

    def dense_copy(j, slot):
        return pltpu.make_async_copy(dense_ref.at[pl.ds(place(j) * GROUP, GROUP)], dense.at[slot], sem_d.at[slot])

    def pair_copy(j, slot):
        return pltpu.make_async_copy(both.at[slot], pair_ref.at[pl.ds(place(j) * GROUP, GROUP)], sem_o.at[slot])

    def item_copy(owner, block, slot, u):
        return pltpu.make_async_copy(
            items[owner].at[pl.ds(block * BLOCK, BLOCK)], raw.at[slot, u], sem_y.at[slot, u]
        )

    def fetch(j, slot):
        dense_copy(j, slot).start()
        for u in range(GROUP):
            where = list_ref[place(j) * GROUP + u] & 65535
            block = where & (blocks - 1)
            owner = where >> (blocks.bit_length() - 1)
            choose(owner, 0, owners, lambda o, u=u, block=block: item_copy(o, block, slot, u).start())

    @pl.when(chunks > 0)
    def _():
        fetch(0, 0)

    high, low = halves(start_ref[...])
    v_high[...] = high.reshape(v_high.shape)
    v_low[...] = low.reshape(v_low.shape)
    out_ref[...] = jnp.zeros_like(out_ref)

    def step(j, carry):
        slot = j & 1

        @pl.when(j + 1 < chunks)
        def _():
            fetch(j + 1, 1 - slot)

        @pl.when(j >= 2)
        def _():
            pair_copy(j - 2, slot).wait()

        dense_copy(j, slot).wait()
        pulled = []
        for u in range(GROUP):
            item_copy(0, 0, slot, u).wait()
            block = list_ref[place(j) * GROUP + u] >> 16
            y_high, y_low = halves(raw[slot, u])
            y_both = jnp.concatenate([y_high, y_low], axis=0)
            both[slot, u] = y_both
            fit, ones = decode(dense[slot, u])
            scores = pair_scores(v_high[block], v_low[block], y_both)
            pulled.append((block, pair_pull(ones + fit * (1.0 - scores), y_both)))
        for block, value in pulled:
            out_ref[block] += value
        pair_copy(j, slot).start()
        return carry

    lax.fori_loop(0, chunks, step, 0)

    @pl.when(chunks >= 2)
    def _():
        pair_copy(chunks - 2, chunks & 1).wait()

    @pl.when(chunks >= 1)
    def _():
        pair_copy(chunks - 1, (chunks - 1) & 1).wait()


def as_column(row, eye):
    return jnp.sum(jnp.where(eye, row, 0.0), axis=1, keepdims=True)


def eye_mask():
    return lax.broadcasted_iota(jnp.int32, (BLOCK, BLOCK), 0) == lax.broadcasted_iota(
        jnp.int32, (BLOCK, BLOCK), 1
    )


def step_kernel(side, first, last, list_ref, total_ref, gram_ref, own_ref, other_ref, dense_ref, pair_ref, *rest):
    given = 1 if first else 3
    states = rest[:given]
    made = 2 if first else 5 if last else 4
    outs = rest[given : given + made]
    dense, both, v_high, v_low, acc, sem_d, sem_y = rest[given + made :]
    chunks = (total_ref[side] + (GROUP - 1)) >> GROUP_BITS
    end = list_ref.shape[0] // GROUP - 1

    def place(j):
        return end - j if side else j

    shape3 = v_high.shape

    def dense_copy(j, slot):
        return pltpu.make_async_copy(dense_ref.at[pl.ds(place(j) * GROUP, GROUP)], dense.at[slot], sem_d.at[slot])

    def pair_copy(j, slot):
        return pltpu.make_async_copy(pair_ref.at[pl.ds(place(j) * GROUP, GROUP)], both.at[slot], sem_y.at[slot])

    def fetch(j, slot):
        dense_copy(j, slot).start()
        pair_copy(j, slot).start()

    @pl.when(chunks > 0)
    def _():
        fetch(0, 0)

    summed = own_ref[...] + other_ref[...]
    gram_high, gram_low = halves(gram_ref[...])
    if first:
        start = states[0][...]
        direction = summed - dot3(start, gram_high, gram_low) - RIDGE * start
        outs[0][...] = direction
    else:
        iterate, residual, direction = (ref[...] for ref in states)
        image = summed + dot3(direction, gram_high, gram_low) + RIDGE * direction
        norm_now = row_dot(residual, residual)
        alpha = norm_now / (row_dot(direction, image) + EPSILON)
        iterate = iterate + alpha * direction
        residual = residual - alpha * image
        norm_next = row_dot(residual, residual)
        direction = residual + norm_next / (norm_now + EPSILON) * direction
        outs[0][...] = iterate
        outs[1][...] = direction
        if last:
            for b in range(shape3[0]):
                rows = slice(b * BLOCK, (b + 1) * BLOCK)
                outs[2][b : b + 1, :] = row_sums(residual[rows] * residual[rows])
                along = dot3(direction[rows], gram_high, gram_low) + RIDGE * direction[rows]
                outs[4][b : b + 1, :] = row_sums(direction[rows] * along)
        else:
            outs[2][...] = residual
    high, low = halves(direction)
    v_high[...] = high.reshape(shape3)
    v_low[...] = low.reshape(shape3)
    acc[...] = jnp.zeros_like(acc)

    def step(j, carry):
        slot = j & 1

        @pl.when(j + 1 < chunks)
        def _():
            fetch(j + 1, 1 - slot)

        dense_copy(j, slot).wait()
        pair_copy(j, slot).wait()
        pulled = []
        for u in range(GROUP):
            block = list_ref[place(j) * GROUP + u] >> 16
            y_both = both[slot, u]
            fit, _ = decode(dense[slot, u])
            scores = pair_scores(v_high[block], v_low[block], y_both)
            weighted = fit * scores
            pulled.append((block, weighted * scores if last else pair_pull(weighted, y_both)))
        for block, value in pulled:
            acc[block] += value
        return carry

    lax.fori_loop(0, chunks, step, 0)
    if last:
        for b in range(shape3[0]):
            outs[3][b : b + 1, :] = row_sums(acc[b])
    else:
        outs[3 if not first else 1][...] = acc[...].reshape(own_ref.shape)


def finish_kernel(slice_rows, sides, place_ref, *rest):
    out_ref, mine_ref = rest[-2:]
    eye = eye_mask()
    done = 0
    for side in range(sides):
        iterate_ref, direction_ref, norm_ref, square_ref, own_ref, other_ref = rest[6 * side : 6 * side + 6]
        curve = own_ref[...] + other_ref[...] + square_ref[...]
        alpha = norm_ref[...] / (curve + EPSILON)
        for b in range(alpha.shape[0]):
            rows = pl.ds(b * BLOCK, BLOCK)
            out_ref[pl.ds(done, BLOCK), :] = (
                iterate_ref[rows, :] + as_column(alpha[b : b + 1, :], eye) * direction_ref[rows, :]
            )
            done += BLOCK
    mine_ref[...] = out_ref[pl.ds(pl.multiple_of(place_ref[1] * slice_rows, 8), slice_rows), :]


def place_kernel(part, slice_rows, sources, place_ref, own_ref, *rest):
    pieces = rest[: len(sources)]
    out_ref = rest[-1]
    z, x = place_ref[0], place_ref[1]
    out_ref[pl.ds(pl.multiple_of(z * part, 8), part), :] = own_ref[...]
    for (mask_z, mask_x), piece in zip(sources, pieces):
        at = (z ^ mask_z) * part + (x ^ mask_x) * slice_rows
        out_ref[pl.ds(pl.multiple_of(at, 8), slice_rows), :] = piece[...]


SMEM = pl.BlockSpec(memory_space=pltpu.SMEM)
VMEM = pl.BlockSpec(memory_space=pltpu.VMEM)
ANY = pl.BlockSpec(memory_space=pl.ANY)


def make_shards(n_row, n_col):
    n_x = 1 << ((n_col.bit_length() - 1) // 2)
    n_z = n_col // n_x

    def swap(value, axis, mask):
        count = n_row if axis == "row" else n_col
        return lax.ppermute(value, axis, [(i, i ^ mask) for i in range(count)])

    def hop(value, pairs):
        return lax.ppermute(value, "col", [(a * n_x + x, b * n_x + x) for a, b in pairs for x in range(n_x)])

    def direct_z(value):
        return [value] + [swap(value, "col", k * n_x) for k in range(1, n_z)]

    def gather_z(value):
        if n_z != 4:
            return direct_z(value)
        near = swap(value, "col", n_x)
        across = swap(value, "col", 3 * n_x)
        middle = hop(near, [(1, 2), (2, 1)])
        ends = hop(across, [(1, 0), (2, 3)])
        return [value, near, middle + ends, across]

    def shards(
        user_factors,
        item_factors,
        fetch_list,
        tile_user,
        tile_slot,
        entry_row,
        entry_col,
        entry_count,
        tile_count,
    ):
        row = lax.axis_index("row")
        col = lax.axis_index("col")
        my_z, my_x = col // n_x, col % n_x
        user_rows = user_factors.shape[0]
        part = user_rows // n_z
        part_blocks = part // BLOCK
        sides = 2 if part_blocks % 2 == 0 else 1
        side_rows = part // sides
        side_blocks = part_blocks // sides
        blocks = item_factors.shape[0] // BLOCK
        users = tile_user[0, 0]
        slots = tile_slot[0, 0]
        tiles = users.shape[0]
        width = entry_row.shape[-1]

        fetched = fetch_list[0, 0]
        peers, cap = fetched.shape
        flat = fetched.reshape(1, -1)
        local = jnp.sum(
            jnp.where(slots[:, None] == jnp.arange(peers * cap, dtype=jnp.int32)[None, :], flat, 0), axis=1
        )
        alive = jnp.arange(tiles, dtype=jnp.int32) < tile_count[0, 0]
        owner = slots // cap
        owner_row, owner_z, owner_x = owner // n_col, owner % n_col // n_x, owner % n_x
        owned = n_row * n_z * blocks
        named = owner_x * owned + (owner_row * n_z + owner_z) * blocks + local
        facts = jnp.stack([users, jnp.where(alive, named, -1).astype(jnp.int32)])
        facts = jnp.pad(facts, ((0, 6), (0, width - tiles)))
        packed = jnp.concatenate([entry_row[0, 0], entry_col[0, 0], entry_count[0, 0], facts], axis=0)
        entries = direct_z(packed)
        entries += [swap(v, "col", k) for k in range(1, n_x) for v in entries]
        slots_all = n_col * tiles + GROUP
        place = jnp.stack([my_z, my_x, (row * n_z + my_z) * blocks]).astype(jnp.int32)

        listed, total, dense = pl.pallas_call(
            lambda *refs: build_kernel(tiles, part_blocks, owned, sides, *refs),
            out_shape=(
                jax.ShapeDtypeStruct((slots_all,), jnp.int32),
                jax.ShapeDtypeStruct((2,), jnp.int32),
                jax.ShapeDtypeStruct((slots_all, BLOCK, BLOCK), F32),
            ),
            in_specs=[SMEM] + [ANY] * n_col,
            out_specs=(SMEM, SMEM, ANY),
            scratch_shapes=[
                pltpu.SMEM((slots_all,), jnp.int32),
                pltpu.SMEM((n_col, 8, BLOCK), jnp.int32),
                pltpu.VMEM((n_col * packed.shape[0], width), jnp.int32),
                pltpu.VMEM((2, GROUP, BLOCK, BLOCK), F32),
                pltpu.SemaphoreType.DMA((2,)),
                pltpu.SemaphoreType.DMA((2, n_col)),
            ],
            name="build",
        )(place, *entries)

        along_z = gather_z(item_factors)
        by_y = [along_z]
        for m in range(1, n_row // 2):
            by_y.append([swap(v, "row", 2 * m) for v in along_z])
        held_items = []
        for group in by_y:
            held_items += [group, [swap(v, "row", 1) for v in group]]
        held_items = [v for group in held_items for v in group]
        gram = jnp.dot(
            item_factors.T, item_factors, precision=lax.Precision.HIGH, preferred_element_type=F32
        )
        for axis, count, mask in (("col", n_x, 1), ("row", n_row, 1), ("col", n_col, n_x)):
            while mask < count:
                gram = gram + swap(gram, axis, mask)
                mask *= 2

        dense_shape = (2, GROUP, BLOCK, BLOCK)
        pair_shape = (2, GROUP, 2 * BLOCK, K)
        half_shape = (side_blocks, BLOCK, K)

        def begin(side):
            start = lax.dynamic_slice(user_factors, (my_z * part + side * side_rows, 0), (side_rows, K))
            terms, pairs = pl.pallas_call(
                lambda *refs: start_kernel(side, n_row * n_z, blocks, *refs),
                out_shape=(
                    jax.ShapeDtypeStruct(half_shape, F32),
                    jax.ShapeDtypeStruct((slots_all, 2 * BLOCK, K), BF16),
                ),
                in_specs=[SMEM, SMEM, VMEM, ANY] + [ANY] * len(held_items),
                out_specs=(VMEM, ANY),
                scratch_shapes=[
                    pltpu.VMEM(dense_shape, F32),
                    pltpu.VMEM((2, GROUP, BLOCK, K), F32),
                    pltpu.VMEM(pair_shape, BF16),
                    pltpu.VMEM(half_shape, BF16),
                    pltpu.VMEM(half_shape, BF16),
                    pltpu.SemaphoreType.DMA((2,)),
                    pltpu.SemaphoreType.DMA((2, GROUP)),
                    pltpu.SemaphoreType.DMA((2,)),
                ],
            )(listed, total, start, dense, *held_items)
            return start, terms.reshape(side_rows, K), pairs

        def shared(value):
            others = [swap(value, "col", k) for k in range(1, n_x)]
            if n_x == 2:
                return value, others[0]
            stacked = jnp.take(jnp.stack([value] + others), my_x ^ jnp.arange(n_x), axis=0)
            return jnp.sum(stacked, axis=0), jnp.zeros_like(value)

        vector = jax.ShapeDtypeStruct((side_rows, K), F32)
        scalars = jax.ShapeDtypeStruct((side_blocks, BLOCK), F32)

        def advance(side, count, value, pairs, states):
            first, last = count == 0, count == ITERS - 1
            own, other = shared(value)
            outs = (vector, vector) if first else (vector, vector, scalars if last else vector)
            outs = outs if first else outs + ((scalars, scalars) if last else (vector,))
            return pl.pallas_call(
                lambda *refs: step_kernel(side, first, last, *refs),
                out_shape=outs,
                in_specs=[SMEM, SMEM, VMEM, VMEM, VMEM, ANY, ANY] + [VMEM] * len(states),
                out_specs=tuple(VMEM for _ in outs),
                scratch_shapes=[
                    pltpu.VMEM(dense_shape, F32),
                    pltpu.VMEM(pair_shape, BF16),
                    pltpu.VMEM(half_shape, BF16),
                    pltpu.VMEM(half_shape, BF16),
                    pltpu.VMEM(half_shape, F32),
                    pltpu.SemaphoreType.DMA((2,)),
                    pltpu.SemaphoreType.DMA((2,)),
                ],
            )(listed, total, gram, own, other, dense, pairs, *states)

        started = [begin(side) for side in range(sides)]
        states = [(start,) for start, _, _ in started]
        values = [terms for _, terms, _ in started]
        for count in range(ITERS):
            for side in range(sides):
                results = advance(side, count, values[side], started[side][2], states[side])
                if count == ITERS - 1:
                    iterate, direction, norms, values[side], squares = results
                    states[side] = (iterate, direction, norms, squares)
                elif count:
                    iterate, direction, residual, values[side] = results
                    states[side] = (iterate, residual, direction)
                else:
                    residual, values[side] = results
                    states[side] = (states[side][0], residual, residual)
        inputs = []
        for side in range(sides):
            inputs += [*states[side], *shared(values[side])]
        slice_rows = part // n_x
        solved, mine = pl.pallas_call(
            lambda *refs: finish_kernel(slice_rows, sides, *refs),
            out_shape=(jax.ShapeDtypeStruct((part, K), F32), jax.ShapeDtypeStruct((slice_rows, K), F32)),
            in_specs=[SMEM] + [VMEM] * len(inputs),
            out_specs=(VMEM, VMEM),
            name="finish",
        )(place, *inputs)

        sources, pieces = [], []
        for mask_z, piece in enumerate(direct_z(mine)):
            if mask_z:
                for mask_x in range(n_x):
                    sources.append((mask_z, mask_x))
                    pieces.append(swap(piece, "col", mask_x) if mask_x else piece)
        return pl.pallas_call(
            lambda *refs: place_kernel(part, slice_rows, sources, *refs),
            out_shape=jax.ShapeDtypeStruct((user_rows, K), F32),
            in_specs=[SMEM] + [VMEM] * (1 + len(pieces)),
            out_specs=VMEM,
            name="place",
        )(place, solved, *pieces)

    return shards


def solution(mesh):
    n_row, n_col = mesh.shape["row"], mesh.shape["col"]
    inner = make_shards(n_row, n_col)

    return jax.shard_map(
        inner,
        mesh=mesh,
        in_specs=(
            P("row", None),
            P(("row", "col"), None),
            P("row", "col", None, None),
            P("row", "col", None),
            P("row", "col", None),
            P("row", "col", None, None),
            P("row", "col", None, None),
            P("row", "col", None, None),
            P("row", "col"),
        ),
        out_specs=P("row", None),
        check_vma=False,
    )
```

profile of v0, /device:TPU:0, one launch (start us, length us, event | category | flops | bytes accessed | tf_op | source)
XLA Modules:
  0.0 222.2 jit_solution(1543973218093190360)
XLA Ops:
  0.0 5.1 %collective-permute-start.14 = (f32[1024,128]{1,0:T(8,128)}, f32[1024,128]{1,0:T(8,128)S(1)}, u32[]{:S(2)}, u32[]{:S(2)}) collective-permute-start(f32[1024,128]{1,0:T(8,128)} %refs_4_.3), channel_id=1, source_target_pairs={{0,6},{1,7},{2,4},{3,5},{4,2},{5,3},{6,0},{7,1},{8,14},{9,15},{10,... | collective-permute-start | bytes 1572872 | tf_op jit(solution)/shard_map/ppermute | solution.py:388
  13.8 4.4 %collective-permute-done.14.refs_7_ = f32[1024,128]{1,0:T(8,128)S(1)} collective-permute-done((f32[1024,128]{1,0:T(8,128)}, f32[1024,128]{1,0:T(8,128)S(1)}, u32[]{:S(2)}, u32[]{:S(2)}) %collective-permute-start.14) | collective-permute-done | bytes 524320 | tf_op jit(solution)/shard_map/ppermute | solution.py:388
  19.4 9.1 %collective-permute-done.12.refs_5_ = f32[1024,128]{1,0:T(8,128)S(1)} collective-permute-done((f32[1024,128]{1,0:T(8,128)}, f32[1024,128]{1,0:T(8,128)S(1)}, u32[]{:S(2)}, u32[]{:S(2)}) %collective-permute-start.12) | collective-permute-done | bytes 524320 | tf_op jit(solution)/shard_map/ppermute | solution.py:388
  32.6 2.7 %collective-permute-done.9 = f32[128,128]{1,0:T(8,128)S(1)} collective-permute-done((f32[128,128]{1,0:T(8,128)S(1)}, f32[128,128]{1,0:T(8,128)S(1)}, u32[]{:S(2)}, u32[]{:S(2)}) %collective-permute-start.9) | collective-permute-done | bytes 65568 | tf_op jit(solution)/shard_map/ppermute | solution.py:388
  35.3 3.6 %collective-permute-start.1 = (s32[104,512]{1,0:T(8,128)S(1)}, s32[104,512]{1,0:T(8,128)S(1)}, u32[]{:S(2)}, u32[]{:S(2)}) collective-permute-start(s32[104,512]{1,0:T(8,128)S(1)} %pad_add_fusion.refs_1_), channel_id=1, source_target_pairs={{0,4},{1,5},{2,6},{3,7},{4,0},{5,1},{6,2},{7,3},{8,12},{9,13},{10,... | collective-permute-start | bytes 638984 | tf_op jit(solution)/shard_map/ppermute | solution.py:388
  40.4 22.3 %collective-permute-done.1.refs_3_ = s32[104,512]{1,0:T(8,128)S(1)} collective-permute-done((s32[104,512]{1,0:T(8,128)S(1)}, s32[104,512]{1,0:T(8,128)S(1)}, u32[]{:S(2)}, u32[]{:S(2)}) %collective-permute-start.1) | collective-permute-done | bytes 213024 | tf_op jit(solution)/shard_map/ppermute | solution.py:388
  62.7 6.6 %collective-permute-done.refs_2_ = s32[104,512]{1,0:T(8,128)S(1)} collective-permute-done((s32[104,512]{1,0:T(8,128)S(1)}, s32[104,512]{1,0:T(8,128)S(1)}, u32[]{:S(2)}, u32[]{:S(2)}) %collective-permute-start) | collective-permute-done | bytes 213024 | tf_op jit(solution)/shard_map/ppermute | solution.py:388
  73.0 4.4 %collective-permute-done.6.refs_8_ = s32[104,512]{1,0:T(8,128)S(1)} collective-permute-done((s32[104,512]{1,0:T(8,128)S(1)}, s32[104,512]{1,0:T(8,128)S(1)}, u32[]{:S(2)}, u32[]{:S(2)}) %collective-permute-start.6) | collective-permute-done | bytes 213024 | tf_op jit(solution)/shard_map/ppermute | solution.py:388
  78.9 3.0 %collective-permute-done.5.refs_7_ = s32[104,512]{1,0:T(8,128)S(1)} collective-permute-done((s32[104,512]{1,0:T(8,128)S(1)}, s32[104,512]{1,0:T(8,128)S(1)}, u32[]{:S(2)}, u32[]{:S(2)}) %collective-permute-start.5) | collective-permute-done | bytes 213024 | tf_op jit(solution)/shard_map/ppermute | solution.py:388
  81.9 2.3 %collective-permute-done.4.refs_6_ = s32[104,512]{1,0:T(8,128)S(1)} collective-permute-done((s32[104,512]{1,0:T(8,128)S(1)}, s32[104,512]{1,0:T(8,128)S(1)}, u32[]{:S(2)}, u32[]{:S(2)}) %collective-permute-start.4) | collective-permute-done | bytes 213024 | tf_op jit(solution)/shard_map/ppermute | solution.py:388
  86.3 3.5 %collective-permute-done.23.refs_15_ = f32[1024,128]{1,0:T(8,128)} collective-permute-done((f32[1024,128]{1,0:T(8,128)S(1)}, f32[1024,128]{1,0:T(8,128)}, u32[]{:S(2)}, u32[]{:S(2)}) %collective-permute-start.23) | collective-permute-done | bytes 524320 | tf_op jit(solution)/shard_map/ppermute | solution.py:388
  90.2 10.7 %collective-permute-done.21.refs_13_ = f32[1024,128]{1,0:T(8,128)} collective-permute-done((f32[1024,128]{1,0:T(8,128)S(1)}, f32[1024,128]{1,0:T(8,128)}, u32[]{:S(2)}, u32[]{:S(2)}) %collective-permute-start.21) | collective-permute-done | bytes 524320 | tf_op jit(solution)/shard_map/ppermute | solution.py:388
  101.0 8.9 %collective-permute-done.22.refs_14_ = f32[1024,128]{1,0:T(8,128)} collective-permute-done((f32[1024,128]{1,0:T(8,128)S(1)}, f32[1024,128]{1,0:T(8,128)}, u32[]{:S(2)}, u32[]{:S(2)}) %collective-permute-start.22) | collective-permute-done | bytes 524320 | tf_op jit(solution)/shard_map/ppermute | solution.py:388
  112.4 9.3 %build.1 = (s32[264]{0:T(512)}, s32[2]{0:T(128)}, f32[264,128,128]{2,1,0:T(8,128)}) custom-call(s32[3]{0:T(128)} %pad_add_fusion.2.refs_0_, s32[104,512]{1,0:T(8,128)} %copy-done.7, s32[104,512]{1,0:T(8,128)} %copy-done.10, s32[104,512]{1,0:T(8,128)} %copy-done.9, s32[104,512]{1,0:T(8,128)} %copy-done.8, s32[104,512]{1,0:T(8,128)} %collective-permute-done.3.refs_5_, ...), custom_call_target="tpu_custom_call" | custom-call | tf_op jit(solution)/shard_map/build/pallas_call | solution.py:450
  122.1 6.6 %shard_map.95 = (f32[2,128,128]{2,1,0:T(8,128)}, bf16[264,256,128]{2,1,0:T(8,128)(2,1)}) custom-call(s32[264]{0:T(512)} %get-tuple-element.36.refs_0_, s32[2]{0:T(128)} %get-tuple-element.37.refs_1_, f32[256,128]{1,0:T(8,128)} %get-tuple-element.67.refs_2_.refs_7_, f32[264,128,128]{2,1,0:T(8,128)} %get-tuple-element.38.refs_3_.refs_5_, f32[1024,128]{1,0:T(8,128)} %refs_4_.3, ...), custom_call_target="tpu_custom_call" | custom-call | tf_op jit(solution)/shard_map/pallas_call | solution.py:492
  128.6 2.3 %collective-permute-start.32 = (f32[256,128]{1,0:T(8,128)}, f32[256,128]{1,0:T(8,128)S(1)}, u32[]{:S(2)}, u32[]{:S(2)}) collective-permute-start(f32[256,128]{1,0:T(8,128)} %bitcast.39), channel_id=1, source_target_pairs={{0,1},{1,0},{2,3},{3,2},{4,5},{5,4},{6,7},{7,6},{8,9},{9,8},{10,11... | collective-permute-start | bytes 393224 | tf_op jit(solution)/shard_map/ppermute | solution.py:388
  130.9 9.1 %shard_map.91 = (f32[2,128,128]{2,1,0:T(8,128)}, bf16[264,256,128]{2,1,0:T(8,128)(2,1)}) custom-call(s32[264]{0:T(512)} %get-tuple-element.36.refs_0_, s32[2]{0:T(128)} %get-tuple-element.37.refs_1_, f32[256,128]{1,0:T(8,128)} %get-tuple-element.68.refs_2_.refs_7_, f32[264,128,128]{2,1,0:T(8,128)} %get-tuple-element.38.refs_3_.refs_5_, f32[1024,128]{1,0:T(8,128)} %refs_4_.3, ...), custom_call_target="tpu_custom_call" | custom-call | tf_op jit(solution)/shard_map/pallas_call | solution.py:492
  140.3 5.2 %collective-permute-done.11 = f32[128,128]{1,0:T(8,128)S(1)} collective-permute-done((f32[128,128]{1,0:T(8,128)S(1)}, f32[128,128]{1,0:T(8,128)S(1)}, u32[]{:S(2)}, u32[]{:S(2)}) %collective-permute-start.11) | collective-permute-done | bytes 65568 | tf_op jit(solution)/shard_map/ppermute | solution.py:388
  146.7 4.5 %shard_map.96 = (f32[256,128]{1,0:T(8,128)}, f32[256,128]{1,0:T(8,128)}) custom-call(s32[264]{0:T(512)} %get-tuple-element.36.refs_0_, s32[2]{0:T(128)} %get-tuple-element.37.refs_1_, f32[128,128]{1,0:T(8,128)} %add.122.refs_2_, f32[256,128]{1,0:T(8,128)} %bitcast.40, f32[256,128]{1,0:T(8,128)} %copy-done.14, ...), custom_call_target="tpu_custom_call" | custom-call | tf_op jit(solution)/shard_map/pallas_call | solution.py:528
  151.2 2.1 collective-permute-start.33
  154.0 6.1 %shard_map.92 = (f32[256,128]{1,0:T(8,128)}, f32[256,128]{1,0:T(8,128)}) custom-call(s32[264]{0:T(512)} %get-tuple-element.36.refs_0_, s32[2]{0:T(128)} %get-tuple-element.37.refs_1_, f32[128,128]{1,0:T(8,128)} %add.122.refs_2_, f32[256,128]{1,0:T(8,128)} %bitcast.38, f32[256,128]{1,0:T(8,128)} %copy-done.16, ...), custom_call_target="tpu_custom_call" | custom-call | tf_op jit(solution)/shard_map/pallas_call | solution.py:528
  160.8 4.8 %shard_map.97 = (f32[256,128]{1,0:T(8,128)}, f32[256,128]{1,0:T(8,128)}, f32[256,128]{1,0:T(8,128)}, f32[256,128]{1,0:T(8,128)}) custom-call(s32[264]{0:T(512)} %get-tuple-element.36.refs_0_, s32[2]{0:T(128)} %get-tuple-element.37.refs_1_, f32[128,128]{1,0:T(8,128)} %add.122.refs_2_, f32[256,128]{1,0:T(8,128)} %get-tuple-element.54.refs_3_, ...), custom_call_target="tpu_custom_call" | custom-call | tf_op jit(solution)/shard_map/pallas_call | solution.py:528
  168.3 6.3 %shard_map.93 = (f32[256,128]{1,0:T(8,128)}, f32[256,128]{1,0:T(8,128)}, f32[256,128]{1,0:T(8,128)}, f32[256,128]{1,0:T(8,128)}) custom-call(s32[264]{0:T(512)} %get-tuple-element.36.refs_0_, s32[2]{0:T(128)} %get-tuple-element.37.refs_1_, f32[128,128]{1,0:T(8,128)} %add.122.refs_2_, f32[256,128]{1,0:T(8,128)} %get-tuple-element.41.refs_3_, ...), custom_call_target="tpu_custom_call" | custom-call | tf_op jit(solution)/shard_map/pallas_call | solution.py:528
  175.3 3.7 %shard_map.98 = (f32[256,128]{1,0:T(8,128)}, f32[256,128]{1,0:T(8,128)}, f32[2,128]{1,0:T(2,128)}, f32[2,128]{1,0:T(2,128)}, f32[2,128]{1,0:T(2,128)}) custom-call(s32[264]{0:T(512)} %get-tuple-element.36.refs_0_, s32[2]{0:T(128)} %get-tuple-element.37.refs_1_, f32[128,128]{1,0:T(8,128)} %add.122.refs_2_, f32[256,128]{1,0:T(8,128)} %get-tuple-element.56.refs_3_, ...), custom_call_target="tpu_custom_call" | custom-call | tf_op jit(solution)/shard_map/pallas_call | solution.py:528
  179.0 2.1 collective-permute-start.35
  181.7 4.6 %shard_map.94 = (f32[256,128]{1,0:T(8,128)}, f32[256,128]{1,0:T(8,128)}, f32[2,128]{1,0:T(2,128)}, f32[2,128]{1,0:T(2,128)}, f32[2,128]{1,0:T(2,128)}) custom-call(s32[264]{0:T(512)} %get-tuple-element.36.refs_0_, s32[2]{0:T(128)} %get-tuple-element.37.refs_1_, f32[128,128]{1,0:T(8,128)} %add.122.refs_2_, f32[256,128]{1,0:T(8,128)} %get-tuple-element.43.refs_3_, ...), custom_call_target="tpu_custom_call" | custom-call | tf_op jit(solution)/shard_map/pallas_call | solution.py:528
  186.4 3.8 %collective-permute-done.31.refs_6_ = f32[2,128]{1,0:T(2,128)S(1)} collective-permute-done((f32[2,128]{1,0:T(2,128)}, f32[2,128]{1,0:T(2,128)S(1)}, u32[]{:S(2)}, u32[]{:S(2)}) %collective-permute-start.31) | collective-permute-done | bytes 1056 | tf_op jit(solution)/shard_map/ppermute | solution.py:388
  192.9 7.9 %collective-permute-start.38 = (f32[256,128]{1,0:T(8,128)}, f32[256,128]{1,0:T(8,128)S(1)}, u32[]{:S(2)}, u32[]{:S(2)}) collective-permute-start(f32[256,128]{1,0:T(8,128)} %get-tuple-element.66), channel_id=1, source_target_pairs={{0,4},{1,5},{2,6},{3,7},{4,0},{5,1},{6,2},{7,3},{8,12},{9,13},{10,... | collective-permute-start | bytes 393224 | tf_op jit(solution)/shard_map/ppermute | solution.py:388
  200.9 9.3 %collective-permute-done.38.refs_4_ = f32[256,128]{1,0:T(8,128)S(1)} collective-permute-done((f32[256,128]{1,0:T(8,128)}, f32[256,128]{1,0:T(8,128)S(1)}, u32[]{:S(2)}, u32[]{:S(2)}) %collective-permute-start.38) | collective-permute-done | bytes 131104 | tf_op jit(solution)/shard_map/ppermute | solution.py:388
  212.2 4.3 %collective-permute-done.39.refs_5_ = f32[256,128]{1,0:T(8,128)S(1)} collective-permute-done((f32[256,128]{1,0:T(8,128)S(1)}, f32[256,128]{1,0:T(8,128)S(1)}, u32[]{:S(2)}, u32[]{:S(2)}) %collective-permute-start.39) | collective-permute-done | bytes 131104 | tf_op jit(solution)/shard_map/ppermute | solution.py:388
  216.6 2.6 %collective-permute-done.37.refs_3_ = f32[256,128]{1,0:T(8,128)S(1)} collective-permute-done((f32[256,128]{1,0:T(8,128)S(1)}, f32[256,128]{1,0:T(8,128)S(1)}, u32[]{:S(2)}, u32[]{:S(2)}) %collective-permute-start.37) | collective-permute-done | bytes 131104 | tf_op jit(solution)/shard_map/ppermute | solution.py:388
  219.8 2.3 %place.1 = f32[2048,128]{1,0:T(8,128)} custom-call(s32[3]{0:T(128)} %pad_add_fusion.2.refs_0_, f32[512,128]{1,0:T(8,128)} %get-tuple-element.65.refs_1_, f32[256,128]{1,0:T(8,128)} %copy-done.22, f32[256,128]{1,0:T(8,128)} %copy-done.25, f32[256,128]{1,0:T(8,128)} %copy-done.21, f32[256,128]{1,0:T(8,128)} %copy-done.24, f32[256,128]{1,0:T(8,128)} %copy-done.20, ...), custom_call_target="tpu_custom_call" | custom-call | tf_op jit(solution)/shard_map/place/pallas_call | solution.py:577
  (132 shorter events, 37.8 us)
Async XLA Ops:
  0.0 18.2 %collective-permute-start.14 = (f32[1024,128]{1,0:T(8,128)}, f32[1024,128]{1,0:T(8,128)S(1)}, u32[]{:S(2)}, u32[]{:S(2)}) collective-permute-start(f32[1024,128]{1,0:T(8,128)} %refs_4_.3), channel_id=1, source_target_pairs={{0,6},{1,7},{2,4},{3,5},{4,2},{5,3},{6,0},{7,1},{8,14},{9,15},{10,... | collective-permute-start | bytes 1572872 | tf_op jit(solution)/shard_map/ppermute | solution.py:388
  5.1 23.5 %collective-permute-start.12 = (f32[1024,128]{1,0:T(8,128)}, f32[1024,128]{1,0:T(8,128)S(1)}, u32[]{:S(2)}, u32[]{:S(2)}) collective-permute-start(f32[1024,128]{1,0:T(8,128)} %refs_4_.3), channel_id=1, source_target_pairs={{0,2},{1,3},{2,0},{3,1},{4,6},{5,7},{6,4},{7,5},{8,10},{9,11},{10,... | collective-permute-start | bytes 1572872 | tf_op jit(solution)/shard_map/ppermute | solution.py:388
  11.3 19.6 %collective-permute-start.8 = (f32[128,128]{1,0:T(8,128)S(1)}, f32[128,128]{1,0:T(8,128)S(1)}, u32[]{:S(2)}, u32[]{:S(2)}) collective-permute-start(f32[128,128]{1,0:T(8,128)S(1)} %add.118), channel_id=1, source_target_pairs={{0,8},{8,0},{16,24},{24,16},{1,9},{9,1},{17,25},{25,17},{2,10},{10... | collective-permute-start | bytes 196616 | tf_op jit(solution)/shard_map/ppermute | solution.py:388
  12.3 26.6 %collective-permute-start.3 = (s32[104,512]{1,0:T(8,128)S(1)}, s32[104,512]{1,0:T(8,128)}, u32[]{:S(2)}, u32[]{:S(2)}) collective-permute-start(s32[104,512]{1,0:T(8,128)S(1)} %pad_add_fusion.refs_1_), channel_id=1, source_target_pairs={{0,1},{1,0},{2,3},{3,2},{4,5},{5,4},{6,7},{7,6},{8,9},{9,8},{10,11... | collective-permute-start | bytes 638984 | tf_op jit(solution)/shard_map/ppermute | solution.py:388
  18.2 52.6 %collective-permute-start.15 = (f32[1024,128]{1,0:T(8,128)S(1)}, f32[1024,128]{1,0:T(8,128)S(1)}, u32[]{:S(2)}, u32[]{:S(2)}) collective-permute-start(f32[1024,128]{1,0:T(8,128)S(1)} %collective-permute-done.14.refs_7_), channel_id=1, source_target_pairs={{2,0},{3,1},{4,6},{5,7},{10,8},{11,9},{12,14},{13,15},{18,16},{19,... | collective-permute-start | bytes 1572872 | tf_op jit(solution)/shard_map/ppermute | solution.py:391
  28.6 42.8 %collective-permute-start.13 = (f32[1024,128]{1,0:T(8,128)S(1)}, f32[1024,128]{1,0:T(8,128)S(1)}, u32[]{:S(2)}, u32[]{:S(2)}) collective-permute-start(f32[1024,128]{1,0:T(8,128)S(1)} %collective-permute-done.12.refs_5_), channel_id=1, source_target_pairs={{2,4},{3,5},{4,2},{5,3},{10,12},{11,13},{12,10},{13,11},{18,20},{1... | collective-permute-start | bytes 1572872 | tf_op jit(solution)/shard_map/ppermute | solution.py:391
  29.2 11.2 %collective-permute-start.2 = (s32[104,512]{1,0:T(8,128)S(1)}, s32[104,512]{1,0:T(8,128)S(1)}, u32[]{:S(2)}, u32[]{:S(2)}) collective-permute-start(s32[104,512]{1,0:T(8,128)S(1)} %pad_add_fusion.refs_1_), channel_id=1, source_target_pairs={{0,6},{1,7},{2,4},{3,5},{4,2},{5,3},{6,0},{7,1},{8,14},{9,15},{10,... | collective-permute-start | bytes 638984 | tf_op jit(solution)/shard_map/ppermute | solution.py:388
  35.3 27.4 %collective-permute-start.1 = (s32[104,512]{1,0:T(8,128)S(1)}, s32[104,512]{1,0:T(8,128)S(1)}, u32[]{:S(2)}, u32[]{:S(2)}) collective-permute-start(s32[104,512]{1,0:T(8,128)S(1)} %pad_add_fusion.refs_1_), channel_id=1, source_target_pairs={{0,4},{1,5},{2,6},{3,7},{4,0},{5,1},{6,2},{7,3},{8,12},{9,13},{10,... | collective-permute-start | bytes 638984 | tf_op jit(solution)/shard_map/ppermute | solution.py:388
  38.9 34.0 %collective-permute-start.20 = (f32[1024,128]{1,0:T(8,128)}, f32[1024,128]{1,0:T(8,128)S(1)}, u32[]{:S(2)}, u32[]{:S(2)}) collective-permute-start(f32[1024,128]{1,0:T(8,128)} %refs_4_.3), channel_id=1, source_target_pairs={{0,16},{8,24},{16,0},{24,8},{1,17},{9,25},{17,1},{25,9},{2,18},{10... | collective-permute-start | bytes 1572872 | tf_op jit(solution)/shard_map/ppermute | solution.py:388
  40.4 45.3 %collective-permute-start.16 = (f32[1024,128]{1,0:T(8,128)}, f32[1024,128]{1,0:T(8,128)S(1)}, u32[]{:S(2)}, u32[]{:S(2)}) collective-permute-start(f32[1024,128]{1,0:T(8,128)} %refs_4_.3), channel_id=1, source_target_pairs={{0,8},{8,0},{16,24},{24,16},{1,9},{9,1},{17,25},{25,17},{2,10},{10... | collective-permute-start | bytes 1572872 | tf_op jit(solution)/shard_map/ppermute | solution.py:388
  69.3 8.1 %collective-permute-start.6 = (s32[104,512]{1,0:T(8,128)S(1)}, s32[104,512]{1,0:T(8,128)S(1)}, u32[]{:S(2)}, u32[]{:S(2)}) collective-permute-start(s32[104,512]{1,0:T(8,128)S(1)} %collective-permute-done.2.refs_4_), channel_id=1, source_target_pairs={{0,1},{1,0},{2,3},{3,2},{4,5},{5,4},{6,7},{7,6},{8,9},{9,8},{10,11... | collective-permute-start | bytes 638984 | tf_op jit(solution)/shard_map/ppermute | solution.py:388
  70.8 11.1 %collective-permute-start.5 = (s32[104,512]{1,0:T(8,128)S(1)}, s32[104,512]{1,0:T(8,128)S(1)}, u32[]{:S(2)}, u32[]{:S(2)}) collective-permute-start(s32[104,512]{1,0:T(8,128)S(1)} %collective-permute-done.1.refs_3_), channel_id=1, source_target_pairs={{0,1},{1,0},{2,3},{3,2},{4,5},{5,4},{6,7},{7,6},{8,9},{9,8},{10,11... | collective-permute-start | bytes 638984 | tf_op jit(solution)/shard_map/ppermute | solution.py:388
  71.3 12.9 %collective-permute-start.4 = (s32[104,512]{1,0:T(8,128)S(1)}, s32[104,512]{1,0:T(8,128)S(1)}, u32[]{:S(2)}, u32[]{:S(2)}) collective-permute-start(s32[104,512]{1,0:T(8,128)S(1)} %collective-permute-done.refs_2_), channel_id=1, source_target_pairs={{0,1},{1,0},{2,3},{3,2},{4,5},{5,4},{6,7},{7,6},{8,9},{9,8},{10,11... | collective-permute-start | bytes 638984 | tf_op jit(solution)/shard_map/ppermute | solution.py:388
  72.9 13.3 %collective-permute-start.24 = (f32[1024,128]{1,0:T(8,128)S(1)}, f32[1024,128]{1,0:T(8,128)S(1)}, u32[]{:S(2)}, u32[]{:S(2)}) collective-permute-start(f32[1024,128]{1,0:T(8,128)S(1)} %collective-permute-done.20.refs_12_), channel_id=1, source_target_pairs={{0,8},{8,0},{16,24},{24,16},{1,9},{9,1},{17,25},{25,17},{2,10},{10... | collective-permute-start | bytes 1572872 | tf_op jit(solution)/shard_map/ppermute | solution.py:388
  77.4 12.3 %collective-permute-start.23 = (f32[1024,128]{1,0:T(8,128)S(1)}, f32[1024,128]{1,0:T(8,128)}, u32[]{:S(2)}, u32[]{:S(2)}) collective-permute-start(f32[1024,128]{1,0:T(8,128)S(1)} %collective-permute-done.14.refs_7_), channel_id=1, source_target_pairs={{0,16},{8,24},{16,0},{24,8},{1,17},{9,25},{17,1},{25,9},{2,18},{10... | collective-permute-start | bytes 1572872 | tf_op jit(solution)/shard_map/ppermute | solution.py:388
  84.2 16.7 %collective-permute-start.21 = (f32[1024,128]{1,0:T(8,128)S(1)}, f32[1024,128]{1,0:T(8,128)}, u32[]{:S(2)}, u32[]{:S(2)}) collective-permute-start(f32[1024,128]{1,0:T(8,128)S(1)} %collective-permute-done.12.refs_5_), channel_id=1, source_target_pairs={{0,16},{8,24},{16,0},{24,8},{1,17},{9,25},{17,1},{25,9},{2,18},{10... | collective-permute-start | bytes 1572872 | tf_op jit(solution)/shard_map/ppermute | solution.py:388
  85.7 24.2 %collective-permute-start.22 = (f32[1024,128]{1,0:T(8,128)S(1)}, f32[1024,128]{1,0:T(8,128)}, u32[]{:S(2)}, u32[]{:S(2)}) collective-permute-start(f32[1024,128]{1,0:T(8,128)S(1)} %add.124.refs_6_), channel_id=1, source_target_pairs={{0,16},{8,24},{16,0},{24,8},{1,17},{9,25},{17,1},{25,9},{2,18},{10... | collective-permute-start | bytes 1572872 | tf_op jit(solution)/shard_map/ppermute | solution.py:388
  86.2 35.4 %collective-permute-start.17 = (f32[1024,128]{1,0:T(8,128)S(1)}, f32[1024,128]{1,0:T(8,128)}, u32[]{:S(2)}, u32[]{:S(2)}) collective-permute-start(f32[1024,128]{1,0:T(8,128)S(1)} %collective-permute-done.12.refs_5_), channel_id=1, source_target_pairs={{0,8},{8,0},{16,24},{24,16},{1,9},{9,1},{17,25},{25,17},{2,10},{10... | collective-permute-start | bytes 1572872 | tf_op jit(solution)/shard_map/ppermute | solution.py:388
  89.7 32.3 %collective-permute-start.18 = (f32[1024,128]{1,0:T(8,128)S(1)}, f32[1024,128]{1,0:T(8,128)}, u32[]{:S(2)}, u32[]{:S(2)}) collective-permute-start(f32[1024,128]{1,0:T(8,128)S(1)} %add.124.refs_6_), channel_id=1, source_target_pairs={{0,8},{8,0},{16,24},{24,16},{1,9},{9,1},{17,25},{25,17},{2,10},{10... | collective-permute-start | bytes 1572872 | tf_op jit(solution)/shard_map/ppermute | solution.py:388
  89.7 32.3 %collective-permute-start.27 = (f32[1024,128]{1,0:T(8,128)}, f32[1024,128]{1,0:T(8,128)}, u32[]{:S(2)}, u32[]{:S(2)}) collective-permute-start(f32[1024,128]{1,0:T(8,128)} %collective-permute-done.23.refs_15_), channel_id=1, source_target_pairs={{0,8},{8,0},{16,24},{24,16},{1,9},{9,1},{17,25},{25,17},{2,10},{10... | collective-permute-start | bytes 1572872 | tf_op jit(solution)/shard_map/ppermute | solution.py:388
  101.0 21.0 %collective-permute-start.25 = (f32[1024,128]{1,0:T(8,128)}, f32[1024,128]{1,0:T(8,128)}, u32[]{:S(2)}, u32[]{:S(2)}) collective-permute-start(f32[1024,128]{1,0:T(8,128)} %collective-permute-done.21.refs_13_), channel_id=1, source_target_pairs={{0,8},{8,0},{16,24},{24,16},{1,9},{9,1},{17,25},{25,17},{2,10},{10... | collective-permute-start | bytes 1572872 | tf_op jit(solution)/shard_map/ppermute | solution.py:388
  109.9 12.1 %collective-permute-start.26 = (f32[1024,128]{1,0:T(8,128)}, f32[1024,128]{1,0:T(8,128)}, u32[]{:S(2)}, u32[]{:S(2)}) collective-permute-start(f32[1024,128]{1,0:T(8,128)} %collective-permute-done.22.refs_14_), channel_id=1, source_target_pairs={{0,8},{8,0},{16,24},{24,16},{1,9},{9,1},{17,25},{25,17},{2,10},{10... | collective-permute-start | bytes 1572872 | tf_op jit(solution)/shard_map/ppermute | solution.py:388
  121.6 18.5 %collective-permute-start.10 = (f32[128,128]{1,0:T(8,128)S(1)}, f32[128,128]{1,0:T(8,128)S(1)}, u32[]{:S(2)}, u32[]{:S(2)}) collective-permute-start(f32[128,128]{1,0:T(8,128)S(1)} %add.120), channel_id=1, source_target_pairs={{0,2},{1,3},{2,0},{3,1},{4,6},{5,7},{6,4},{7,5},{8,10},{9,11},{10,... | collective-permute-start | bytes 196616 | tf_op jit(solution)/shard_map/ppermute | solution.py:388
  128.6 17.4 %collective-permute-start.32 = (f32[256,128]{1,0:T(8,128)}, f32[256,128]{1,0:T(8,128)S(1)}, u32[]{:S(2)}, u32[]{:S(2)}) collective-permute-start(f32[256,128]{1,0:T(8,128)} %bitcast.39), channel_id=1, source_target_pairs={{0,1},{1,0},{2,3},{3,2},{4,5},{5,4},{6,7},{7,6},{8,9},{9,8},{10,11... | collective-permute-start | bytes 393224 | tf_op jit(solution)/shard_map/ppermute | solution.py:388
  140.1 13.2 %collective-permute-start.28 = (f32[256,128]{1,0:T(8,128)}, f32[256,128]{1,0:T(8,128)S(1)}, u32[]{:S(2)}, u32[]{:S(2)}) collective-permute-start(f32[256,128]{1,0:T(8,128)} %bitcast.37), channel_id=1, source_target_pairs={{0,1},{1,0},{2,3},{3,2},{4,5},{5,4},{6,7},{7,6},{8,9},{9,8},{10,11... | collective-permute-start | bytes 393224 | tf_op jit(solution)/shard_map/ppermute | solution.py:388
  151.2 8.9 %collective-permute-start.33 = (f32[256,128]{1,0:T(8,128)}, f32[256,128]{1,0:T(8,128)S(1)}, u32[]{:S(2)}, u32[]{:S(2)}) collective-permute-start(f32[256,128]{1,0:T(8,128)} %get-tuple-element.54.refs_3_), channel_id=1, source_target_pairs={{0,1},{1,0},{2,3},{3,2},{4,5},{5,4},{6,7},{7,6},{8,9},{9,8},{10,11... | collective-permute-start | bytes 393224 | tf_op jit(solution)/shard_map/ppermute | solution.py:388
  165.6 9.1 %collective-permute-start.34 = (f32[256,128]{1,0:T(8,128)}, f32[256,128]{1,0:T(8,128)S(1)}, u32[]{:S(2)}, u32[]{:S(2)}) collective-permute-start(f32[256,128]{1,0:T(8,128)} %get-tuple-element.56.refs_3_), channel_id=1, source_target_pairs={{0,1},{1,0},{2,3},{3,2},{4,5},{5,4},{6,7},{7,6},{8,9},{9,8},{10,11... | collective-permute-start | bytes 393224 | tf_op jit(solution)/shard_map/ppermute | solution.py:388
  192.7 8.1 %collective-permute-start.40 = (f32[256,128]{1,0:T(8,128)}, f32[256,128]{1,0:T(8,128)S(1)}, u32[]{:S(2)}, u32[]{:S(2)}) collective-permute-start(f32[256,128]{1,0:T(8,128)} %get-tuple-element.66), channel_id=1, source_target_pairs={{0,6},{1,7},{2,4},{3,5},{4,2},{5,3},{6,0},{7,1},{8,14},{9,15},{10,... | collective-permute-start | bytes 393224 | tf_op jit(solution)/shard_map/ppermute | solution.py:388
  192.9 17.3 %collective-permute-start.38 = (f32[256,128]{1,0:T(8,128)}, f32[256,128]{1,0:T(8,128)S(1)}, u32[]{:S(2)}, u32[]{:S(2)}) collective-permute-start(f32[256,128]{1,0:T(8,128)} %get-tuple-element.66), channel_id=1, source_target_pairs={{0,4},{1,5},{2,6},{3,7},{4,0},{5,1},{6,2},{7,3},{8,12},{9,13},{10,... | collective-permute-start | bytes 393224 | tf_op jit(solution)/shard_map/ppermute | solution.py:388
  200.8 10.3 %collective-permute-start.36 = (f32[256,128]{1,0:T(8,128)}, f32[256,128]{1,0:T(8,128)S(1)}, u32[]{:S(2)}, u32[]{:S(2)}) collective-permute-start(f32[256,128]{1,0:T(8,128)} %get-tuple-element.66), channel_id=1, source_target_pairs={{0,2},{1,3},{2,0},{3,1},{4,6},{5,7},{6,4},{7,5},{8,10},{9,11},{10,... | collective-permute-start | bytes 393224 | tf_op jit(solution)/shard_map/ppermute | solution.py:388
  200.9 11.4 %collective-permute-start.41 = (f32[256,128]{1,0:T(8,128)S(1)}, f32[256,128]{1,0:T(8,128)S(1)}, u32[]{:S(2)}, u32[]{:S(2)}) collective-permute-start(f32[256,128]{1,0:T(8,128)S(1)} %collective-permute-done.40.refs_6_), channel_id=1, source_target_pairs={{0,1},{1,0},{2,3},{3,2},{4,5},{5,4},{6,7},{7,6},{8,9},{9,8},{10,11... | collective-permute-start | bytes 393224 | tf_op jit(solution)/shard_map/ppermute | solution.py:388
  211.1 8.1 %collective-permute-start.37 = (f32[256,128]{1,0:T(8,128)S(1)}, f32[256,128]{1,0:T(8,128)S(1)}, u32[]{:S(2)}, u32[]{:S(2)}) collective-permute-start(f32[256,128]{1,0:T(8,128)S(1)} %collective-permute-done.36.refs_2_), channel_id=1, source_target_pairs={{0,1},{1,0},{2,3},{3,2},{4,5},{5,4},{6,7},{7,6},{8,9},{9,8},{10,11... | collective-permute-start | bytes 393224 | tf_op jit(solution)/shard_map/ppermute | solution.py:388
  (38 other events, 845.8 us)
where the time goes:
time: 223 us; the launch traced here: 222 us
  waiting for transfers between devices  103 us (46%)
  Pallas kernels  59.2 us (27%)
  starting transfers between devices  45.6 us (20%)
  local copies, waits for them, and re-layouts  6.86 us (3%)
  other arithmetic  4.48 us (2%)
    ppermute x40, waiting for transfers between devices, swap(): return lax.ppermute(value, axis, [(i, i ^ mask) for i in range(count)])  103 us
    ppermute x40, starting transfers between devices, swap(): return lax.ppermute(value, axis, [(i, i ^ mask) for i in range(count)])  43.7 us
    pallas_call x6, Pallas kernels, advance(): pl.pallas_call(lambda *refs: step_kernel(side, first, last, *refs), out_s...  29.9 us
    pallas_call x2, Pallas kernels, begin(): pl.pallas_call(lambda *refs: start_kernel(side, n_row * n_z, blocks, *ref...  15.7 us
    pallas_call x1, Pallas kernels, shards(): pl.pallas_call(lambda *refs: build_kernel(tiles, part_blocks, owned, side...  9.27 us
    unnamed x56, local copies, waits for them, and re-layouts  5.15 us
  transfers between devices with their start and end apart: 42, of which 16 were waited for; matrix products, arithmetic and copies ran while one was open for 4% of the time, Pallas kernels for 25%

commit v1 on v0

--- a/solution.py
+++ b/solution.py
@@ -120,7 +120,7 @@
     ids = lax.broadcasted_iota(jnp.int32, (BLOCK, entry_ref.shape[1]), 0)
 
     def out_copy(chunk, slot):
-        return pltpu.make_async_copy(buf.at[slot], dense_ref.at[pl.ds(chunk * GROUP, GROUP)], sem.at[slot])
+        return pltpu.make_async_copy(buf.at[slot], own_chunk(dense_ref, chunk), sem.at[slot])
 
     def step(j, carry):
         slot = j & 1
@@ -159,6 +159,25 @@
         out_copy(0, (every - 1) & 1).wait()
 
 
+def own_chunk(ref, chunk):
+    return ref.at[pl.ds(chunk * GROUP, GROUP)]
+
+
+def read_chunk(ref, chunk, scratch):
+    if not scratch:
+        return own_chunk(ref, chunk)
+    pltpu.sync_copy(own_chunk(ref, chunk), scratch[0])
+    return scratch[0]
+
+
+def near(value):
+    return pltpu.with_memory_space_constraint(value, pltpu.VMEM)
+
+
+def far(value):
+    return pltpu.with_memory_space_constraint(value, pltpu.HBM)
+
+
 def choose(value, low, high, act):
     if high - low == 1:
         act(low)
@@ -174,80 +193,75 @@
         choose(value, middle, high, act)
 
 
-def start_kernel(side, owners, blocks, list_ref, total_ref, start_ref, dense_ref, *rest):
+def bring_kernel(list_ref, total_ref, dense_ref, kept_ref, sem):
+    chunks = [(total_ref[side] + (GROUP - 1)) >> GROUP_BITS for side in range(2)]
+
+    def dense_copy(j):
+        chunk = jnp.where(j < chunks[0], j, list_ref.shape[0] // GROUP - 1 - (j - chunks[0]))
+        return pltpu.make_async_copy(own_chunk(dense_ref, chunk), own_chunk(kept_ref, chunk), sem.at[j])
+
+    def begin(j, carry):
+        dense_copy(j).start()
+        return carry
+
+    def end(j, carry):
+        dense_copy(j).wait()
+        return carry
+
+    lax.fori_loop(0, chunks[0] + chunks[1], begin, 0)
+    lax.fori_loop(0, chunks[0] + chunks[1], end, 0)
+
+
+def gather_kernel(owners, blocks, list_ref, total_ref, *rest):
     items = rest[:owners]
-    out_ref, pair_ref = rest[owners : owners + 2]
-    dense, raw, both, v_high, v_low, sem_d, sem_y, sem_o = rest[owners + 2 :]
+    pair_ref = rest[owners]
+    buf = rest[owners + 1 :]
+    front, back = (((total_ref[side] + (GROUP - 1)) >> GROUP_BITS) << GROUP_BITS for side in range(2))
+    slots = list_ref.shape[0]
+
+    def step(j, carry):
+        at = jnp.where(j < front, j, slots - back + (j - front))
+        where = list_ref[at] & 65535
+        rows = pl.ds(pl.multiple_of((where & (blocks - 1)) * BLOCK, BLOCK), BLOCK)
+        target = buf[0] if buf else pair_ref.at[at]
+
+        def split(owner):
+            high, low = halves(items[owner][rows, :])
+            target[:BLOCK, :] = high
+            target[BLOCK:, :] = low
+
+        choose(where >> (blocks.bit_length() - 1), 0, owners, split)
+        if buf:
+            pltpu.sync_copy(target, pair_ref.at[at])
+        return carry
+
+    lax.fori_loop(0, front + back, step, 0)
+
+
+def start_kernel(side, list_ref, total_ref, start_ref, dense_ref, pair_ref, out_ref, v_high, v_low, *copies):
     chunks = (total_ref[side] + (GROUP - 1)) >> GROUP_BITS
     end = list_ref.shape[0] // GROUP - 1
-
-    def place(j):
-        return end - j if side else j
-
-    def dense_copy(j, slot):
-        return pltpu.make_async_copy(dense_ref.at[pl.ds(place(j) * GROUP, GROUP)], dense.at[slot], sem_d.at[slot])
-
-    def pair_copy(j, slot):
-        return pltpu.make_async_copy(both.at[slot], pair_ref.at[pl.ds(place(j) * GROUP, GROUP)], sem_o.at[slot])
-
-    def item_copy(owner, block, slot, u):
-        return pltpu.make_async_copy(
-            items[owner].at[pl.ds(block * BLOCK, BLOCK)], raw.at[slot, u], sem_y.at[slot, u]
-        )
-
-    def fetch(j, slot):
-        dense_copy(j, slot).start()
-        for u in range(GROUP):
-            where = list_ref[place(j) * GROUP + u] & 65535
-            block = where & (blocks - 1)
-            owner = where >> (blocks.bit_length() - 1)
-            choose(owner, 0, owners, lambda o, u=u, block=block: item_copy(o, block, slot, u).start())
-
-    @pl.when(chunks > 0)
-    def _():
-        fetch(0, 0)
-
     high, low = halves(start_ref[...])
     v_high[...] = high.reshape(v_high.shape)
     v_low[...] = low.reshape(v_low.shape)
     out_ref[...] = jnp.zeros_like(out_ref)
 
     def step(j, carry):
-        slot = j & 1
-
-        @pl.when(j + 1 < chunks)
-        def _():
-            fetch(j + 1, 1 - slot)
-
-        @pl.when(j >= 2)
-        def _():
-            pair_copy(j - 2, slot).wait()
-
-        dense_copy(j, slot).wait()
+        chunk = end - j if side else j
+        dense = read_chunk(dense_ref, chunk, copies[:1])
+        both = read_chunk(pair_ref, chunk, copies[1:])
         pulled = []
         for u in range(GROUP):
-            item_copy(0, 0, slot, u).wait()
-            block = list_ref[place(j) * GROUP + u] >> 16
-            y_high, y_low = halves(raw[slot, u])
-            y_both = jnp.concatenate([y_high, y_low], axis=0)
-            both[slot, u] = y_both
-            fit, ones = decode(dense[slot, u])
+            block = list_ref[chunk * GROUP + u] >> 16
+            y_both = both[u]
+            fit, ones = decode(dense[u])
             scores = pair_scores(v_high[block], v_low[block], y_both)
             pulled.append((block, pair_pull(ones + fit * (1.0 - scores), y_both)))
         for block, value in pulled:
             out_ref[block] += value
-        pair_copy(j, slot).start()
         return carry
 
     lax.fori_loop(0, chunks, step, 0)
-
-    @pl.when(chunks >= 2)
-    def _():
-        pair_copy(chunks - 2, chunks & 1).wait()
-
-    @pl.when(chunks >= 1)
-    def _():
-        pair_copy(chunks - 1, (chunks - 1) & 1).wait()
 
 
 def as_column(row, eye):
@@ -265,29 +279,10 @@
     states = rest[:given]
     made = 2 if first else 5 if last else 4
     outs = rest[given : given + made]
-    dense, both, v_high, v_low, acc, sem_d, sem_y = rest[given + made :]
+    v_high, v_low, acc, *copies = rest[given + made :]
+    shape3 = v_high.shape
     chunks = (total_ref[side] + (GROUP - 1)) >> GROUP_BITS
     end = list_ref.shape[0] // GROUP - 1
-
-    def place(j):
-        return end - j if side else j
-
-    shape3 = v_high.shape
-
-    def dense_copy(j, slot):
-        return pltpu.make_async_copy(dense_ref.at[pl.ds(place(j) * GROUP, GROUP)], dense.at[slot], sem_d.at[slot])
-
-    def pair_copy(j, slot):
-        return pltpu.make_async_copy(pair_ref.at[pl.ds(place(j) * GROUP, GROUP)], both.at[slot], sem_y.at[slot])
-
-    def fetch(j, slot):
-        dense_copy(j, slot).start()
-        pair_copy(j, slot).start()
-
-    @pl.when(chunks > 0)
-    def _():
-        fetch(0, 0)
-
     summed = own_ref[...] + other_ref[...]
     gram_high, gram_low = halves(gram_ref[...])
     if first:
@@ -319,19 +314,14 @@
     acc[...] = jnp.zeros_like(acc)
 
     def step(j, carry):
-        slot = j & 1
-
-        @pl.when(j + 1 < chunks)
-        def _():
-            fetch(j + 1, 1 - slot)
-
-        dense_copy(j, slot).wait()
-        pair_copy(j, slot).wait()
+        chunk = end - j if side else j
+        dense = read_chunk(dense_ref, chunk, copies[:1])
+        both = read_chunk(pair_ref, chunk, copies[1:])
         pulled = []
         for u in range(GROUP):
-            block = list_ref[place(j) * GROUP + u] >> 16
-            y_both = both[slot, u]
-            fit, _ = decode(dense[slot, u])
+            block = list_ref[chunk * GROUP + u] >> 16
+            y_both = both[u]
+            fit, _ = decode(dense[u])
             scores = pair_scores(v_high[block], v_low[block], y_both)
             weighted = fit * scores
             pulled.append((block, weighted * scores if last else pair_pull(weighted, y_both)))
@@ -442,9 +432,14 @@
         facts = jnp.stack([users, jnp.where(alive, named, -1).astype(jnp.int32)])
         facts = jnp.pad(facts, ((0, 6), (0, width - tiles)))
         packed = jnp.concatenate([entry_row[0, 0], entry_col[0, 0], entry_count[0, 0], facts], axis=0)
-        entries = direct_z(packed)
+        entries = gather_z(packed)
         entries += [swap(v, "col", k) for k in range(1, n_x) for v in entries]
         slots_all = n_col * tiles + GROUP
+        resident = slots_all * BLOCK * K * 8 <= 40 << 20
+        limit = pltpu.CompilerParams(vmem_limit_bytes=(8 if resident else 24) << 20)
+        hold, keep = (pltpu.VMEM, near) if resident else (pltpu.HBM, far)
+        wide = VMEM if resident else ANY
+        copied = [] if resident else [pltpu.VMEM((GROUP, BLOCK, BLOCK), F32), pltpu.VMEM((GROUP, 2 * BLOCK, K), BF16)]
         place = jnp.stack([my_z, my_x, (row * n_z + my_z) * blocks]).astype(jnp.int32)
 
         listed, total, dense = pl.pallas_call(
@@ -452,7 +447,7 @@
             out_shape=(
                 jax.ShapeDtypeStruct((slots_all,), jnp.int32),
                 jax.ShapeDtypeStruct((2,), jnp.int32),
-                jax.ShapeDtypeStruct((slots_all, BLOCK, BLOCK), F32),
+                pltpu.HBM((slots_all, BLOCK, BLOCK), F32),
             ),
             in_specs=[SMEM] + [ANY] * n_col,
             out_specs=(SMEM, SMEM, ANY),
@@ -464,6 +459,7 @@
                 pltpu.SemaphoreType.DMA((2,)),
                 pltpu.SemaphoreType.DMA((2, n_col)),
             ],
+            compiler_params=limit,
             name="build",
         )(place, *entries)
 
@@ -483,32 +479,38 @@
                 gram = gram + swap(gram, axis, mask)
                 mask *= 2
 
-        dense_shape = (2, GROUP, BLOCK, BLOCK)
-        pair_shape = (2, GROUP, 2 * BLOCK, K)
+        if resident:
+            dense = pl.pallas_call(
+                bring_kernel,
+                out_shape=pltpu.VMEM((slots_all, BLOCK, BLOCK), F32),
+                in_specs=[SMEM, SMEM, ANY],
+                out_specs=VMEM,
+                scratch_shapes=[pltpu.SemaphoreType.DMA((slots_all // GROUP,))],
+                compiler_params=limit,
+                name="bring",
+            )(listed, total, far(dense))
+        pairs = pl.pallas_call(
+            lambda *refs: gather_kernel(n_row * n_z, blocks, *refs),
+            out_shape=hold((slots_all, 2 * BLOCK, K), BF16),
+            in_specs=[SMEM, SMEM] + [VMEM] * len(held_items),
+            out_specs=wide,
+            scratch_shapes=[] if resident else [pltpu.VMEM((2 * BLOCK, K), BF16)],
+            compiler_params=limit,
+            name="gather",
+        )(listed, total, *(near(v) for v in held_items))
         half_shape = (side_blocks, BLOCK, K)
 
         def begin(side):
             start = lax.dynamic_slice(user_factors, (my_z * part + side * side_rows, 0), (side_rows, K))
-            terms, pairs = pl.pallas_call(
-                lambda *refs: start_kernel(side, n_row * n_z, blocks, *refs),
-                out_shape=(
-                    jax.ShapeDtypeStruct(half_shape, F32),
-                    jax.ShapeDtypeStruct((slots_all, 2 * BLOCK, K), BF16),
-                ),
-                in_specs=[SMEM, SMEM, VMEM, ANY] + [ANY] * len(held_items),
-                out_specs=(VMEM, ANY),
-                scratch_shapes=[
-                    pltpu.VMEM(dense_shape, F32),
-                    pltpu.VMEM((2, GROUP, BLOCK, K), F32),
-                    pltpu.VMEM(pair_shape, BF16),
-                    pltpu.VMEM(half_shape, BF16),
-                    pltpu.VMEM(half_shape, BF16),
-                    pltpu.SemaphoreType.DMA((2,)),
-                    pltpu.SemaphoreType.DMA((2, GROUP)),
-                    pltpu.SemaphoreType.DMA((2,)),
-                ],
-            )(listed, total, start, dense, *held_items)
-            return start, terms.reshape(side_rows, K), pairs
+            terms = pl.pallas_call(
+                lambda *refs: start_kernel(side, *refs),
+                out_shape=pltpu.VMEM(half_shape, F32),
+                in_specs=[SMEM, SMEM, VMEM, wide, wide],
+                out_specs=VMEM,
+                scratch_shapes=[pltpu.VMEM(half_shape, BF16), pltpu.VMEM(half_shape, BF16)] + copied,
+                compiler_params=limit,
+            )(listed, total, near(start), keep(dense), keep(pairs))
+            return start, terms.reshape(side_rows, K)
 
         def shared(value):
             others = [swap(value, "col", k) for k in range(1, n_x)]
@@ -517,10 +519,10 @@
             stacked = jnp.take(jnp.stack([value] + others), my_x ^ jnp.arange(n_x), axis=0)
             return jnp.sum(stacked, axis=0), jnp.zeros_like(value)
 
-        vector = jax.ShapeDtypeStruct((side_rows, K), F32)
-        scalars = jax.ShapeDtypeStruct((side_blocks, BLOCK), F32)
-
-        def advance(side, count, value, pairs, states):
+        vector = pltpu.VMEM((side_rows, K), F32)
+        scalars = pltpu.VMEM((side_blocks, BLOCK), F32)
+
+        def advance(side, count, value, states):
             first, last = count == 0, count == ITERS - 1
             own, other = shared(value)
             outs = (vector, vector) if first else (vector, vector, scalars if last else vector)
@@ -528,25 +530,23 @@
             return pl.pallas_call(
                 lambda *refs: step_kernel(side, first, last, *refs),
                 out_shape=outs,
-                in_specs=[SMEM, SMEM, VMEM, VMEM, VMEM, ANY, ANY] + [VMEM] * len(states),
+                in_specs=[SMEM, SMEM, VMEM, VMEM, VMEM, wide, wide] + [VMEM] * len(states),
                 out_specs=tuple(VMEM for _ in outs),
                 scratch_shapes=[
-                    pltpu.VMEM(dense_shape, F32),
-                    pltpu.VMEM(pair_shape, BF16),
                     pltpu.VMEM(half_shape, BF16),
                     pltpu.VMEM(half_shape, BF16),
                     pltpu.VMEM(half_shape, F32),
-                    pltpu.SemaphoreType.DMA((2,)),
-                    pltpu.SemaphoreType.DMA((2,)),
-                ],
-            )(listed, total, gram, own, other, dense, pairs, *states)
+                ]
+                + copied,
+                compiler_params=limit,
+            )(listed, total, near(gram), near(own), near(other), keep(dense), keep(pairs), *(near(v) for v in states))
 
         started = [begin(side) for side in range(sides)]
-        states = [(start,) for start, _, _ in started]
-        values = [terms for _, terms, _ in started]
+        states = [(start,) for start, _ in started]
+        values = [terms for _, terms in started]
         for count in range(ITERS):
             for side in range(sides):
-                results = advance(side, count, values[side], started[side][2], states[side])
+                results = advance(side, count, values[side], states[side])
                 if count == ITERS - 1:
                     iterate, direction, norms, values[side], squares = results
                     states[side] = (iterate, direction, norms, squares)
@@ -562,11 +562,12 @@
         slice_rows = part // n_x
         solved, mine = pl.pallas_call(
             lambda *refs: finish_kernel(slice_rows, sides, *refs),
-            out_shape=(jax.ShapeDtypeStruct((part, K), F32), jax.ShapeDtypeStruct((slice_rows, K), F32)),
+            out_shape=(pltpu.VMEM((part, K), F32), pltpu.VMEM((slice_rows, K), F32)),
             in_specs=[SMEM] + [VMEM] * len(inputs),
             out_specs=(VMEM, VMEM),
+            compiler_params=limit,
             name="finish",
-        )(place, *inputs)
+        )(place, *(near(v) for v in inputs))
 
         sources, pieces = [], []
         for mask_z, piece in enumerate(direct_z(mine)):
@@ -579,8 +580,9 @@
             out_shape=jax.ShapeDtypeStruct((user_rows, K), F32),
             in_specs=[SMEM] + [VMEM] * (1 + len(pieces)),
             out_specs=VMEM,
+            compiler_params=limit,
             name="place",
-        )(place, solved, *pieces)
+        )(place, near(solved), *(near(v) for v in pieces))
 
     return shards
 

time: 223 us -> 194 us (0.87)
  waiting for transfers between devices: 103 us -> 75.2 us
  Pallas kernels: 59.2 us -> 41.5 us
  starting transfers between devices: 45.6 us -> 61.1 us
    ppermute x40 -> x39, waiting for transfers between devices: 103 us -> 72.2 us  [swap(): return lax.ppermute(value, axis, [(i, i ^ mask) for i in range(count)])]
    ppermute x40 -> x39, starting transfers between devices: 43.7 us -> 57.2 us  [swap(): return lax.ppermute(value, axis, [(i, i ^ mask) for i in range(count)])]
    pallas_call x6, Pallas kernels: 29.9 us -> 17.6 us  [advance(): pl.pallas_call(lambda *refs: step_kernel(side, first, last, *refs), out_s...]
    pallas_call x2 -> x4, Pallas kernels: 15.7 us -> 11.3 us  [the longest x2 5.77 us: begin(): pl.pallas_call(lambda *refs: start_kernel(side, *refs), out_shape=pltpu.V...]
    ppermute x2 -> x4, waiting for transfers between devices: 0.01 us -> 2.98 us  [hop(): lax.ppermute(value, 'col', [(a * n_x + x, b * n_x + x) for a, b in pairs...]
    unnamed x56 -> x28, local copies, waits for them, and re-layouts: 5.15 us -> 7.4 us
  transfers between devices with their start and end apart: 42 -> 43, of which waited for: 16 -> 18; matrix products, arithmetic and copies ran while one was open for 4% -> 4% of each run, Pallas kernels for 25% -> 20%
where the time goes in v1:
time: 194 us; the launch traced here: 193 us
  waiting for transfers between devices  75.2 us (39%)
  starting transfers between devices  61.1 us (31%)
  Pallas kernels  41.5 us (21%)
  local copies, waits for them, and re-layouts  8.39 us (4%)
  other arithmetic  4.17 us (2%)
    ppermute x39, waiting for transfers between devices, swap(): return lax.ppermute(value, axis, [(i, i ^ mask) for i in range(count)])  72.2 us
    ppermute x39, starting transfers between devices, swap(): return lax.ppermute(value, axis, [(i, i ^ mask) for i in range(count)])  57.2 us
    pallas_call x6, Pallas kernels, advance(): pl.pallas_call(lambda *refs: step_kernel(side, first, last, *refs), out_s...  17.6 us
    pallas_call x1, Pallas kernels, shards(): pl.pallas_call(lambda *refs: build_kernel(tiles, part_blocks, owned, side...  10.2 us
    unnamed x28, local copies, waits for them, and re-layouts  7.4 us
    pallas_call x2, Pallas kernels, begin(): pl.pallas_call(lambda *refs: start_kernel(side, *refs), out_shape=pltpu.V...  5.77 us
    ppermute x4, starting transfers between devices, hop(): lax.ppermute(value, 'col', [(a * n_x + x, b * n_x + x) for a, b in pairs...  3.92 us
  transfers between devices with their start and end apart: 43, of which 18 were waited for; matrix products, arithmetic and copies ran while one was open for 4% of the time, Pallas kernels for 20%

profile of v1, /device:TPU:0, one launch (start us, length us, event | category | flops | bytes accessed | tf_op | source)
XLA Modules:
  0.0 193.2 jit_solution(193525599601049933)
XLA Ops:
  0.0 5.1 %collective-permute-start.15 = (f32[1024,128]{1,0:T(8,128)}, f32[1024,128]{1,0:T(8,128)S(1)}, u32[]{:S(2)}, u32[]{:S(2)}) collective-permute-start(f32[1024,128]{1,0:T(8,128)} %refs_2_.1), channel_id=1, source_target_pairs={{0,6},{1,7},{2,4},{3,5},{4,2},{5,3},{6,0},{7,1},{8,14},{9,15},{10,... | collective-permute-start | bytes 1572872 | tf_op jit(solution)/shard_map/ppermute | solution.py:378
  14.9 3.3 %collective-permute-done.15.refs_5_ = f32[1024,128]{1,0:T(8,128)S(1)} collective-permute-done((f32[1024,128]{1,0:T(8,128)}, f32[1024,128]{1,0:T(8,128)S(1)}, u32[]{:S(2)}, u32[]{:S(2)}) %collective-permute-start.15) | collective-permute-done | bytes 524320 | tf_op jit(solution)/shard_map/ppermute | solution.py:378
  21.2 11.8 %collective-permute-start = (s32[104,512]{1,0:T(8,128)S(1)}, s32[104,512]{1,0:T(8,128)S(1)}, u32[]{:S(2)}, u32[]{:S(2)}) collective-permute-start(s32[104,512]{1,0:T(8,128)S(1)} %pad_add_fusion.refs_1_), channel_id=1, source_target_pairs={{0,2},{1,3},{2,0},{3,1},{4,6},{5,7},{6,4},{7,5},{8,10},{9,11},{10,... | collective-permute-start | bytes 638984 | tf_op jit(solution)/shard_map/ppermute | solution.py:378
  35.1 13.9 %collective-permute-done.refs_2_ = s32[104,512]{1,0:T(8,128)S(1)} collective-permute-done((s32[104,512]{1,0:T(8,128)S(1)}, s32[104,512]{1,0:T(8,128)S(1)}, u32[]{:S(2)}, u32[]{:S(2)}) %collective-permute-start) | collective-permute-done | bytes 213024 | tf_op jit(solution)/shard_map/ppermute | solution.py:378
  50.5 3.0 %collective-permute-done.3 = s32[104,512]{1,0:T(8,128)S(1)} collective-permute-done((s32[104,512]{1,0:T(8,128)S(1)}, s32[104,512]{1,0:T(8,128)S(1)}, u32[]{:S(2)}, u32[]{:S(2)}) %collective-permute-start.3) | collective-permute-done | bytes 213024 | tf_op jit(solution)/shard_map/ppermute | solution.py:381
  57.9 4.5 %collective-permute-done.7.refs_8_ = s32[104,512]{1,0:T(8,128)S(1)} collective-permute-done((s32[104,512]{1,0:T(8,128)S(1)}, s32[104,512]{1,0:T(8,128)S(1)}, u32[]{:S(2)}, u32[]{:S(2)}) %collective-permute-start.7) | collective-permute-done | bytes 213024 | tf_op jit(solution)/shard_map/ppermute | solution.py:378
  64.5 2.4 %collective-permute-done.5.refs_6_ = s32[104,512]{1,0:T(8,128)S(1)} collective-permute-done((s32[104,512]{1,0:T(8,128)S(1)}, s32[104,512]{1,0:T(8,128)S(1)}, u32[]{:S(2)}, u32[]{:S(2)}) %collective-permute-start.5) | collective-permute-done | bytes 213024 | tf_op jit(solution)/shard_map/ppermute | solution.py:378
  72.7 5.2 %collective-permute-done.24.refs_13_ = f32[1024,128]{1,0:T(8,128)} collective-permute-done((f32[1024,128]{1,0:T(8,128)S(1)}, f32[1024,128]{1,0:T(8,128)}, u32[]{:S(2)}, u32[]{:S(2)}) %collective-permute-start.24) | collective-permute-done | bytes 524320 | tf_op jit(solution)/shard_map/ppermute | solution.py:378
  79.3 9.9 %collective-permute-done.22.refs_11_ = f32[1024,128]{1,0:T(8,128)} collective-permute-done((f32[1024,128]{1,0:T(8,128)S(1)}, f32[1024,128]{1,0:T(8,128)}, u32[]{:S(2)}, u32[]{:S(2)}) %collective-permute-start.22) | collective-permute-done | bytes 524320 | tf_op jit(solution)/shard_map/ppermute | solution.py:378
  90.5 7.2 %collective-permute-done.23.refs_12_ = f32[1024,128]{1,0:T(8,128)} collective-permute-done((f32[1024,128]{1,0:T(8,128)S(1)}, f32[1024,128]{1,0:T(8,128)}, u32[]{:S(2)}, u32[]{:S(2)}) %collective-permute-start.23) | collective-permute-done | bytes 524320 | tf_op jit(solution)/shard_map/ppermute | solution.py:378
  103.4 10.2 %build.1 = (s32[264]{0:T(512)S(1)}, s32[2]{0:T(128)S(1)}, f32[264,128,128]{2,1,0:T(8,128)}) custom-call(s32[3]{0:T(128)S(1)} %pad_add_fusion.2.refs_0_, s32[104,512]{1,0:T(8,128)S(1)} %pad_add_fusion.refs_1_, s32[104,512]{1,0:T(8,128)S(1)} %copy-done.6, s32[104,512]{1,0:T(8,128)S(1)} %add.121.refs_3_, s32[104,512]{1,0:T(8,128)S(1)} %collective-permute-done.2.refs_4_, ...), custom_call_target="tpu_custom_call" | custom-call | tf_op jit(solution)/shard_map/build/pallas_call | solution.py:445
  113.6 2.2 %bring.1.refs_3_.refs_5_ = f32[264,128,128]{2,1,0:T(8,128)S(1)} custom-call(s32[264]{0:T(512)S(1)} %get-tuple-element.32.list_ref.refs_0_, s32[2]{0:T(128)S(1)} %get-tuple-element.33.total_ref.refs_1_, f32[264,128,128]{2,1,0:T(8,128)} %get-tuple-element.34.dense_ref), custom_call_target="tpu_custom_call" | custom-call | tf_op jit(solution)/shard_map/bring/pallas_call | solution.py:483
  115.9 6.2 %collective-permute-start.11 = (f32[128,128]{1,0:T(8,128)S(1)}, f32[128,128]{1,0:T(8,128)S(1)}, u32[]{:S(2)}, u32[]{:S(2)}) collective-permute-start(f32[128,128]{1,0:T(8,128)S(1)} %add.124), channel_id=1, source_target_pairs={{0,2},{1,3},{2,0},{3,1},{4,6},{5,7},{6,4},{7,5},{8,10},{9,11},{10,... | collective-permute-start | bytes 196616 | tf_op jit(solution)/shard_map/ppermute | solution.py:378
  122.2 3.3 %gather.1.refs_4_.refs_6_ = bf16[264,256,128]{2,1,0:T(8,128)(2,1)S(1)} custom-call(s32[264]{0:T(512)S(1)} %get-tuple-element.32.list_ref.refs_0_, s32[2]{0:T(128)S(1)} %get-tuple-element.33.total_ref.refs_1_, f32[1024,128]{1,0:T(8,128)S(1)} %copy-done, f32[1024,128]{1,0:T(8,128)S(1)} %collective-permute-done.13.refs_3_, f32[1024,128]{1,0:T(8,128)S(1)} %add.128.refs_4_, ...), custom_call_target="tpu_custom_call" | custom-call | tf_op jit(solution)/shard_map/gather/pallas_call | solution.py:492
  125.5 3.7 %shard_map.91 = f32[2,128,128]{2,1,0:T(8,128)S(1)} custom-call(s32[264]{0:T(512)S(1)} %get-tuple-element.32.list_ref.refs_0_, s32[2]{0:T(128)S(1)} %get-tuple-element.33.total_ref.refs_1_, f32[256,128]{1,0:T(8,128)S(1)} %get-tuple-element.60.refs_2_.refs_7_, f32[264,128,128]{2,1,0:T(8,128)S(1)} %bring.1.refs_3_.refs_5_, ...), custom_call_target="tpu_custom_call" | custom-call | tf_op jit(solution)/shard_map/pallas_call | solution.py:505
  129.3 2.1 %shard_map.95 = f32[2,128,128]{2,1,0:T(8,128)S(1)} custom-call(s32[264]{0:T(512)S(1)} %get-tuple-element.32.list_ref.refs_0_, s32[2]{0:T(128)S(1)} %get-tuple-element.33.total_ref.refs_1_, f32[256,128]{1,0:T(8,128)S(1)} %get-tuple-element.59.refs_2_.refs_7_, f32[264,128,128]{2,1,0:T(8,128)S(1)} %bring.1.refs_3_.refs_5_, ...), custom_call_target="tpu_custom_call" | custom-call | tf_op jit(solution)/shard_map/pallas_call | solution.py:505
  131.4 2.1 %collective-permute-start.33 = (f32[256,128]{1,0:T(8,128)S(1)}, f32[256,128]{1,0:T(8,128)S(1)}, u32[]{:S(2)}, u32[]{:S(2)}) collective-permute-start(f32[256,128]{1,0:T(8,128)S(1)} %bitcast.37), channel_id=1, source_target_pairs={{0,1},{1,0},{2,3},{3,2},{4,5},{5,4},{6,7},{7,6},{8,9},{9,8},{10,11... | collective-permute-start | bytes 393224 | tf_op jit(solution)/shard_map/ppermute | solution.py:378
  133.5 7.0 %collective-permute-done.12 = f32[128,128]{1,0:T(8,128)S(1)} collective-permute-done((f32[128,128]{1,0:T(8,128)S(1)}, f32[128,128]{1,0:T(8,128)S(1)}, u32[]{:S(2)}, u32[]{:S(2)}) %collective-permute-start.12) | collective-permute-done | bytes 65568 | tf_op jit(solution)/shard_map/ppermute | solution.py:378
  140.6 3.8 %shard_map.92 = (f32[256,128]{1,0:T(8,128)S(1)}, f32[256,128]{1,0:T(8,128)S(1)}) custom-call(s32[264]{0:T(512)S(1)} %get-tuple-element.32.list_ref.refs_0_, s32[2]{0:T(128)S(1)} %get-tuple-element.33.total_ref.refs_1_, f32[128,128]{1,0:T(8,128)S(1)} %add.126.refs_2_, f32[256,128]{1,0:T(8,128)S(1)} %bitcast.40, ...), custom_call_target="tpu_custom_call" | custom-call | tf_op jit(solution)/shard_map/pallas_call | solution.py:530
  144.5 2.3 %shard_map.96 = (f32[256,128]{1,0:T(8,128)S(1)}, f32[256,128]{1,0:T(8,128)S(1)}) custom-call(s32[264]{0:T(512)S(1)} %get-tuple-element.32.list_ref.refs_0_, s32[2]{0:T(128)S(1)} %get-tuple-element.33.total_ref.refs_1_, f32[128,128]{1,0:T(8,128)S(1)} %add.126.refs_2_, f32[256,128]{1,0:T(8,128)S(1)} %bitcast.38, ...), custom_call_target="tpu_custom_call" | custom-call | tf_op jit(solution)/shard_map/pallas_call | solution.py:530
  146.8 2.1 %collective-permute-start.34 = (f32[256,128]{1,0:T(8,128)S(1)}, f32[256,128]{1,0:T(8,128)S(1)}, u32[]{:S(2)}, u32[]{:S(2)}) collective-permute-start(f32[256,128]{1,0:T(8,128)S(1)} %get-tuple-element.46.refs_3_), channel_id=1, source_target_pairs={{0,1},{1,0},{2,3},{3,2},{4,5},{5,4},{6,7},{7,6},{8,9},{9,8},{10,11... | collective-permute-start | bytes 393224 | tf_op jit(solution)/shard_map/ppermute | solution.py:378
  150.0 4.1 %shard_map.93 = (f32[256,128]{1,0:T(8,128)S(1)}, f32[256,128]{1,0:T(8,128)S(1)}, f32[256,128]{1,0:T(8,128)S(1)}, f32[256,128]{1,0:T(8,128)S(1)}) custom-call(s32[264]{0:T(512)S(1)} %get-tuple-element.32.list_ref.refs_0_, s32[2]{0:T(128)S(1)} %get-tuple-element.33.total_ref.refs_1_, f32[128,128]{1,0:T(8,128)S(1)} %add.126.refs_2_, ...), custom_call_target="tpu_custom_call" | custom-call | tf_op jit(solution)/shard_map/pallas_call | solution.py:530
  154.3 2.8 %shard_map.97 = (f32[256,128]{1,0:T(8,128)S(1)}, f32[256,128]{1,0:T(8,128)S(1)}, f32[256,128]{1,0:T(8,128)S(1)}, f32[256,128]{1,0:T(8,128)S(1)}) custom-call(s32[264]{0:T(512)S(1)} %get-tuple-element.32.list_ref.refs_0_, s32[2]{0:T(128)S(1)} %get-tuple-element.33.total_ref.refs_1_, f32[128,128]{1,0:T(8,128)S(1)} %add.126.refs_2_, ...), custom_call_target="tpu_custom_call" | custom-call | tf_op jit(solution)/shard_map/pallas_call | solution.py:530
  157.1 2.1 %collective-permute-start.35 = (f32[256,128]{1,0:T(8,128)S(1)}, f32[256,128]{1,0:T(8,128)S(1)}, u32[]{:S(2)}, u32[]{:S(2)}) collective-permute-start(f32[256,128]{1,0:T(8,128)S(1)} %get-tuple-element.48.refs_3_), channel_id=1, source_target_pairs={{0,1},{1,0},{2,3},{3,2},{4,5},{5,4},{6,7},{7,6},{8,9},{9,8},{10,11... | collective-permute-start | bytes 393224 | tf_op jit(solution)/shard_map/ppermute | solution.py:378
  159.6 2.5 %shard_map.94 = (f32[256,128]{1,0:T(8,128)S(1)}, f32[256,128]{1,0:T(8,128)S(1)}, f32[2,128]{1,0:T(2,128)S(1)}, f32[2,128]{1,0:T(2,128)S(1)}, f32[2,128]{1,0:T(2,128)S(1)}) custom-call(s32[264]{0:T(512)S(1)} %get-tuple-element.32.list_ref.refs_0_, s32[2]{0:T(128)S(1)} %get-tuple-element.33.total_ref.refs_1_, f32[128,128]{1,0:T(8,128)S(1)} %add.126.refs_2_, ...), custom_call_target="tpu_custom_call" | custom-call | tf_op jit(solution)/shard_map/pallas_call | solution.py:530
  163.0 2.0 %shard_map.98 = (f32[256,128]{1,0:T(8,128)S(1)}, f32[256,128]{1,0:T(8,128)S(1)}, f32[2,128]{1,0:T(2,128)S(1)}, f32[2,128]{1,0:T(2,128)S(1)}, f32[2,128]{1,0:T(2,128)S(1)}) custom-call(s32[264]{0:T(512)S(1)} %get-tuple-element.32.list_ref.refs_0_, s32[2]{0:T(128)S(1)} %get-tuple-element.33.total_ref.refs_1_, f32[128,128]{1,0:T(8,128)S(1)} %add.126.refs_2_, ...), custom_call_target="tpu_custom_call" | custom-call | tf_op jit(solution)/shard_map/pallas_call | solution.py:530
  165.0 2.3 %collective-permute-start.36 = (f32[2,128]{1,0:T(2,128)S(1)}, f32[2,128]{1,0:T(2,128)S(1)}, u32[]{:S(2)}, u32[]{:S(2)}) collective-permute-start(f32[2,128]{1,0:T(2,128)S(1)} %get-tuple-element.56.refs_11_), channel_id=1, source_target_pairs={{0,1},{1,0},{2,3},{3,2},{4,5},{5,4},{6,7},{7,6},{8,9},{9,8},{10,11... | collective-permute-start | bytes 3080 | tf_op jit(solution)/shard_map/ppermute | solution.py:378
  169.9 2.4 %collective-permute-start.39 = (f32[256,128]{1,0:T(8,128)S(1)}, f32[256,128]{1,0:T(8,128)S(1)}, u32[]{:S(2)}, u32[]{:S(2)}) collective-permute-start(f32[256,128]{1,0:T(8,128)S(1)} %get-tuple-element.58), channel_id=1, source_target_pairs={{0,4},{1,5},{2,6},{3,7},{4,0},{5,1},{6,2},{7,3},{8,12},{9,13},{10,... | collective-permute-start | bytes 393224 | tf_op jit(solution)/shard_map/ppermute | solution.py:378
  174.0 3.9 %collective-permute-done.41.refs_6_ = f32[256,128]{1,0:T(8,128)S(1)} collective-permute-done((f32[256,128]{1,0:T(8,128)S(1)}, f32[256,128]{1,0:T(8,128)S(1)}, u32[]{:S(2)}, u32[]{:S(2)}) %collective-permute-start.41) | collective-permute-done | bytes 131104 | tf_op jit(solution)/shard_map/ppermute | solution.py:378
  180.0 3.7 %collective-permute-done.39.refs_4_ = f32[256,128]{1,0:T(8,128)S(1)} collective-permute-done((f32[256,128]{1,0:T(8,128)S(1)}, f32[256,128]{1,0:T(8,128)S(1)}, u32[]{:S(2)}, u32[]{:S(2)}) %collective-permute-start.39) | collective-permute-done | bytes 131104 | tf_op jit(solution)/shard_map/ppermute | solution.py:378
  183.6 2.0 %collective-permute-start.40 = (f32[256,128]{1,0:T(8,128)S(1)}, f32[256,128]{1,0:T(8,128)S(1)}, u32[]{:S(2)}, u32[]{:S(2)}) collective-permute-start(f32[256,128]{1,0:T(8,128)S(1)} %collective-permute-done.39.refs_4_), channel_id=1, source_target_pairs={{0,1},{1,0},{2,3},{3,2},{4,5},{5,4},{6,7},{7,6},{8,9},{9,8},{10,11... | collective-permute-start | bytes 393224 | tf_op jit(solution)/shard_map/ppermute | solution.py:378
  185.7 4.3 %collective-permute-done.40.refs_5_ = f32[256,128]{1,0:T(8,128)S(1)} collective-permute-done((f32[256,128]{1,0:T(8,128)S(1)}, f32[256,128]{1,0:T(8,128)S(1)}, u32[]{:S(2)}, u32[]{:S(2)}) %collective-permute-start.40) | collective-permute-done | bytes 131104 | tf_op jit(solution)/shard_map/ppermute | solution.py:378
  (109 shorter events, 48.6 us)
Async XLA Ops:
  0.0 18.2 %collective-permute-start.15 = (f32[1024,128]{1,0:T(8,128)}, f32[1024,128]{1,0:T(8,128)S(1)}, u32[]{:S(2)}, u32[]{:S(2)}) collective-permute-start(f32[1024,128]{1,0:T(8,128)} %refs_2_.1), channel_id=1, source_target_pairs={{0,6},{1,7},{2,4},{3,5},{4,2},{5,3},{6,0},{7,1},{8,14},{9,15},{10,... | collective-permute-start | bytes 1572872 | tf_op jit(solution)/shard_map/ppermute | solution.py:378
  5.1 27.9 %collective-permute-start.13 = (f32[1024,128]{1,0:T(8,128)}, f32[1024,128]{1,0:T(8,128)S(1)}, u32[]{:S(2)}, u32[]{:S(2)}) collective-permute-start(f32[1024,128]{1,0:T(8,128)} %refs_2_.1), channel_id=1, source_target_pairs={{0,2},{1,3},{2,0},{3,1},{4,6},{5,7},{6,4},{7,5},{8,10},{9,11},{10,... | collective-permute-start | bytes 1572872 | tf_op jit(solution)/shard_map/ppermute | solution.py:378
  12.3 21.4 %collective-permute-start.2 = (s32[104,512]{1,0:T(8,128)S(1)}, s32[104,512]{1,0:T(8,128)S(1)}, u32[]{:S(2)}, u32[]{:S(2)}) collective-permute-start(s32[104,512]{1,0:T(8,128)S(1)} %pad_add_fusion.refs_1_), channel_id=1, source_target_pairs={{0,6},{1,7},{2,4},{3,5},{4,2},{5,3},{6,0},{7,1},{8,14},{9,15},{10,... | collective-permute-start | bytes 638984 | tf_op jit(solution)/shard_map/ppermute | solution.py:378
  13.3 7.9 %collective-permute-start.10 = (f32[128,128]{1,0:T(8,128)S(1)}, f32[128,128]{1,0:T(8,128)S(1)}, u32[]{:S(2)}, u32[]{:S(2)}) collective-permute-start(f32[128,128]{1,0:T(8,128)S(1)} %add.123), channel_id=1, source_target_pairs={{0,16},{8,24},{16,0},{24,8},{1,17},{9,25},{17,1},{25,9},{2,18},{10... | collective-permute-start | bytes 196616 | tf_op jit(solution)/shard_map/ppermute | solution.py:378
  18.2 37.6 %collective-permute-start.16 = (f32[1024,128]{1,0:T(8,128)S(1)}, f32[1024,128]{1,0:T(8,128)S(1)}, u32[]{:S(2)}, u32[]{:S(2)}) collective-permute-start(f32[1024,128]{1,0:T(8,128)S(1)} %collective-permute-done.15.refs_5_), channel_id=1, source_target_pairs={{2,0},{3,1},{4,6},{5,7},{10,8},{11,9},{12,14},{13,15},{18,16},{19,... | collective-permute-start | bytes 1572872 | tf_op jit(solution)/shard_map/ppermute | solution.py:381
  19.4 15.6 %collective-permute-start.4 = (s32[104,512]{1,0:T(8,128)S(1)}, s32[104,512]{1,0:T(8,128)S(1)}, u32[]{:S(2)}, u32[]{:S(2)}) collective-permute-start(s32[104,512]{1,0:T(8,128)S(1)} %pad_add_fusion.refs_1_), channel_id=1, source_target_pairs={{0,1},{1,0},{2,3},{3,2},{4,5},{5,4},{6,7},{7,6},{8,9},{9,8},{10,11... | collective-permute-start | bytes 638984 | tf_op jit(solution)/shard_map/ppermute | solution.py:378
  21.2 27.9 %collective-permute-start = (s32[104,512]{1,0:T(8,128)S(1)}, s32[104,512]{1,0:T(8,128)S(1)}, u32[]{:S(2)}, u32[]{:S(2)}) collective-permute-start(s32[104,512]{1,0:T(8,128)S(1)} %pad_add_fusion.refs_1_), channel_id=1, source_target_pairs={{0,2},{1,3},{2,0},{3,1},{4,6},{5,7},{6,4},{7,5},{8,10},{9,11},{10,... | collective-permute-start | bytes 638984 | tf_op jit(solution)/shard_map/ppermute | solution.py:378
  33.0 23.3 %collective-permute-start.14 = (f32[1024,128]{1,0:T(8,128)S(1)}, f32[1024,128]{1,0:T(8,128)S(1)}, u32[]{:S(2)}, u32[]{:S(2)}) collective-permute-start(f32[1024,128]{1,0:T(8,128)S(1)} %collective-permute-done.13.refs_3_), channel_id=1, source_target_pairs={{2,4},{3,5},{4,2},{5,3},{10,12},{11,13},{12,10},{13,11},{18,20},{1... | collective-permute-start | bytes 1572872 | tf_op jit(solution)/shard_map/ppermute | solution.py:381
  33.7 19.8 %collective-permute-start.3 = (s32[104,512]{1,0:T(8,128)S(1)}, s32[104,512]{1,0:T(8,128)S(1)}, u32[]{:S(2)}, u32[]{:S(2)}) collective-permute-start(s32[104,512]{1,0:T(8,128)S(1)} %collective-permute-done.2.refs_4_), channel_id=1, source_target_pairs={{2,0},{3,1},{4,6},{5,7},{10,8},{11,9},{12,14},{13,15},{18,16},{19,... | collective-permute-start | bytes 638984 | tf_op jit(solution)/shard_map/ppermute | solution.py:381
  35.1 32.6 %collective-permute-start.17 = (f32[1024,128]{1,0:T(8,128)}, f32[1024,128]{1,0:T(8,128)S(1)}, u32[]{:S(2)}, u32[]{:S(2)}) collective-permute-start(f32[1024,128]{1,0:T(8,128)} %refs_2_.1), channel_id=1, source_target_pairs={{0,8},{8,0},{16,24},{24,16},{1,9},{9,1},{17,25},{25,17},{2,10},{10... | collective-permute-start | bytes 1572872 | tf_op jit(solution)/shard_map/ppermute | solution.py:378
  49.0 20.1 %collective-permute-start.21 = (f32[1024,128]{1,0:T(8,128)}, f32[1024,128]{1,0:T(8,128)S(1)}, u32[]{:S(2)}, u32[]{:S(2)}) collective-permute-start(f32[1024,128]{1,0:T(8,128)} %refs_2_.1), channel_id=1, source_target_pairs={{0,16},{8,24},{16,0},{24,8},{1,17},{9,25},{17,1},{25,9},{2,18},{10... | collective-permute-start | bytes 1572872 | tf_op jit(solution)/shard_map/ppermute | solution.py:378
  54.2 8.2 %collective-permute-start.7 = (s32[104,512]{1,0:T(8,128)S(1)}, s32[104,512]{1,0:T(8,128)S(1)}, u32[]{:S(2)}, u32[]{:S(2)}) collective-permute-start(s32[104,512]{1,0:T(8,128)S(1)} %collective-permute-done.2.refs_4_), channel_id=1, source_target_pairs={{0,1},{1,0},{2,3},{3,2},{4,5},{5,4},{6,7},{7,6},{8,9},{9,8},{10,11... | collective-permute-start | bytes 638984 | tf_op jit(solution)/shard_map/ppermute | solution.py:378
  55.7 11.2 %collective-permute-start.5 = (s32[104,512]{1,0:T(8,128)S(1)}, s32[104,512]{1,0:T(8,128)S(1)}, u32[]{:S(2)}, u32[]{:S(2)}) collective-permute-start(s32[104,512]{1,0:T(8,128)S(1)} %collective-permute-done.refs_2_), channel_id=1, source_target_pairs={{0,1},{1,0},{2,3},{3,2},{4,5},{5,4},{6,7},{7,6},{8,9},{9,8},{10,11... | collective-permute-start | bytes 638984 | tf_op jit(solution)/shard_map/ppermute | solution.py:378
  56.3 14.2 %collective-permute-start.6 = (s32[104,512]{1,0:T(8,128)S(1)}, s32[104,512]{1,0:T(8,128)S(1)}, u32[]{:S(2)}, u32[]{:S(2)}) collective-permute-start(s32[104,512]{1,0:T(8,128)S(1)} %add.121.refs_3_), channel_id=1, source_target_pairs={{0,1},{1,0},{2,3},{3,2},{4,5},{5,4},{6,7},{7,6},{8,9},{9,8},{10,11... | collective-permute-start | bytes 638984 | tf_op jit(solution)/shard_map/ppermute | solution.py:378
  63.1 14.9 %collective-permute-start.24 = (f32[1024,128]{1,0:T(8,128)S(1)}, f32[1024,128]{1,0:T(8,128)}, u32[]{:S(2)}, u32[]{:S(2)}) collective-permute-start(f32[1024,128]{1,0:T(8,128)S(1)} %collective-permute-done.15.refs_5_), channel_id=1, source_target_pairs={{0,16},{8,24},{16,0},{24,8},{1,17},{9,25},{17,1},{25,9},{2,18},{10... | collective-permute-start | bytes 1572872 | tf_op jit(solution)/shard_map/ppermute | solution.py:378
  67.6 10.4 %collective-permute-start.20 = (f32[1024,128]{1,0:T(8,128)S(1)}, f32[1024,128]{1,0:T(8,128)S(1)}, u32[]{:S(2)}, u32[]{:S(2)}) collective-permute-start(f32[1024,128]{1,0:T(8,128)S(1)} %collective-permute-done.15.refs_5_), channel_id=1, source_target_pairs={{0,8},{8,0},{16,24},{24,16},{1,9},{9,1},{17,25},{25,17},{2,10},{10... | collective-permute-start | bytes 1572872 | tf_op jit(solution)/shard_map/ppermute | solution.py:378
  67.6 21.6 %collective-permute-start.22 = (f32[1024,128]{1,0:T(8,128)S(1)}, f32[1024,128]{1,0:T(8,128)}, u32[]{:S(2)}, u32[]{:S(2)}) collective-permute-start(f32[1024,128]{1,0:T(8,128)S(1)} %collective-permute-done.13.refs_3_), channel_id=1, source_target_pairs={{0,16},{8,24},{16,0},{24,8},{1,17},{9,25},{17,1},{25,9},{2,18},{10... | collective-permute-start | bytes 1572872 | tf_op jit(solution)/shard_map/ppermute | solution.py:378
  69.1 20.1 %collective-permute-start.18 = (f32[1024,128]{1,0:T(8,128)S(1)}, f32[1024,128]{1,0:T(8,128)S(1)}, u32[]{:S(2)}, u32[]{:S(2)}) collective-permute-start(f32[1024,128]{1,0:T(8,128)S(1)} %collective-permute-done.13.refs_3_), channel_id=1, source_target_pairs={{0,8},{8,0},{16,24},{24,16},{1,9},{9,1},{17,25},{25,17},{2,10},{10... | collective-permute-start | bytes 1572872 | tf_op jit(solution)/shard_map/ppermute | solution.py:378
  71.3 26.4 %collective-permute-start.23 = (f32[1024,128]{1,0:T(8,128)S(1)}, f32[1024,128]{1,0:T(8,128)}, u32[]{:S(2)}, u32[]{:S(2)}) collective-permute-start(f32[1024,128]{1,0:T(8,128)S(1)} %add.128.refs_4_), channel_id=1, source_target_pairs={{0,16},{8,24},{16,0},{24,8},{1,17},{9,25},{17,1},{25,9},{2,18},{10... | collective-permute-start | bytes 1572872 | tf_op jit(solution)/shard_map/ppermute | solution.py:378
  78.0 37.9 %collective-permute-start.25 = (f32[1024,128]{1,0:T(8,128)S(1)}, f32[1024,128]{1,0:T(8,128)}, u32[]{:S(2)}, u32[]{:S(2)}) collective-permute-start(f32[1024,128]{1,0:T(8,128)S(1)} %collective-permute-done.21.refs_10_), channel_id=1, source_target_pairs={{0,8},{8,0},{16,24},{24,16},{1,9},{9,1},{17,25},{25,17},{2,10},{10... | collective-permute-start | bytes 1572872 | tf_op jit(solution)/shard_map/ppermute | solution.py:378
  78.8 43.3 %collective-permute-start.19 = (f32[1024,128]{1,0:T(8,128)S(1)}, f32[1024,128]{1,0:T(8,128)}, u32[]{:S(2)}, u32[]{:S(2)}) collective-permute-start(f32[1024,128]{1,0:T(8,128)S(1)} %add.128.refs_4_), channel_id=1, source_target_pairs={{0,8},{8,0},{16,24},{24,16},{1,9},{9,1},{17,25},{25,17},{2,10},{10... | collective-permute-start | bytes 1572872 | tf_op jit(solution)/shard_map/ppermute | solution.py:378
  89.2 32.9 %collective-permute-start.28 = (f32[1024,128]{1,0:T(8,128)}, f32[1024,128]{1,0:T(8,128)}, u32[]{:S(2)}, u32[]{:S(2)}) collective-permute-start(f32[1024,128]{1,0:T(8,128)} %collective-permute-done.24.refs_13_), channel_id=1, source_target_pairs={{0,8},{8,0},{16,24},{24,16},{1,9},{9,1},{17,25},{25,17},{2,10},{10... | collective-permute-start | bytes 1572872 | tf_op jit(solution)/shard_map/ppermute | solution.py:378
  90.0 32.1 %collective-permute-start.26 = (f32[1024,128]{1,0:T(8,128)}, f32[1024,128]{1,0:T(8,128)}, u32[]{:S(2)}, u32[]{:S(2)}) collective-permute-start(f32[1024,128]{1,0:T(8,128)} %collective-permute-done.22.refs_11_), channel_id=1, source_target_pairs={{0,8},{8,0},{16,24},{24,16},{1,9},{9,1},{17,25},{25,17},{2,10},{10... | collective-permute-start | bytes 1572872 | tf_op jit(solution)/shard_map/ppermute | solution.py:378
  97.7 24.4 %collective-permute-start.27 = (f32[1024,128]{1,0:T(8,128)}, f32[1024,128]{1,0:T(8,128)}, u32[]{:S(2)}, u32[]{:S(2)}) collective-permute-start(f32[1024,128]{1,0:T(8,128)} %collective-permute-done.23.refs_12_), channel_id=1, source_target_pairs={{0,8},{8,0},{16,24},{24,16},{1,9},{9,1},{17,25},{25,17},{2,10},{10... | collective-permute-start | bytes 1572872 | tf_op jit(solution)/shard_map/ppermute | solution.py:378
  115.9 17.6 %collective-permute-start.11 = (f32[128,128]{1,0:T(8,128)S(1)}, f32[128,128]{1,0:T(8,128)S(1)}, u32[]{:S(2)}, u32[]{:S(2)}) collective-permute-start(f32[128,128]{1,0:T(8,128)S(1)} %add.124), channel_id=1, source_target_pairs={{0,2},{1,3},{2,0},{3,1},{4,6},{5,7},{6,4},{7,5},{8,10},{9,11},{10,... | collective-permute-start | bytes 196616 | tf_op jit(solution)/shard_map/ppermute | solution.py:378
  129.2 11.4 %collective-permute-start.29 = (f32[256,128]{1,0:T(8,128)S(1)}, f32[256,128]{1,0:T(8,128)S(1)}, u32[]{:S(2)}, u32[]{:S(2)}) collective-permute-start(f32[256,128]{1,0:T(8,128)S(1)} %bitcast.39), channel_id=1, source_target_pairs={{0,1},{1,0},{2,3},{3,2},{4,5},{5,4},{6,7},{7,6},{8,9},{9,8},{10,11... | collective-permute-start | bytes 393224 | tf_op jit(solution)/shard_map/ppermute | solution.py:378
  131.4 13.1 %collective-permute-start.33 = (f32[256,128]{1,0:T(8,128)S(1)}, f32[256,128]{1,0:T(8,128)S(1)}, u32[]{:S(2)}, u32[]{:S(2)}) collective-permute-start(f32[256,128]{1,0:T(8,128)S(1)} %bitcast.37), channel_id=1, source_target_pairs={{0,1},{1,0},{2,3},{3,2},{4,5},{5,4},{6,7},{7,6},{8,9},{9,8},{10,11... | collective-permute-start | bytes 393224 | tf_op jit(solution)/shard_map/ppermute | solution.py:378
  146.8 7.4 %collective-permute-start.34 = (f32[256,128]{1,0:T(8,128)S(1)}, f32[256,128]{1,0:T(8,128)S(1)}, u32[]{:S(2)}, u32[]{:S(2)}) collective-permute-start(f32[256,128]{1,0:T(8,128)S(1)} %get-tuple-element.46.refs_3_), channel_id=1, source_target_pairs={{0,1},{1,0},{2,3},{3,2},{4,5},{5,4},{6,7},{7,6},{8,9},{9,8},{10,11... | collective-permute-start | bytes 393224 | tf_op jit(solution)/shard_map/ppermute | solution.py:378
  169.6 8.3 %collective-permute-start.41 = (f32[256,128]{1,0:T(8,128)S(1)}, f32[256,128]{1,0:T(8,128)S(1)}, u32[]{:S(2)}, u32[]{:S(2)}) collective-permute-start(f32[256,128]{1,0:T(8,128)S(1)} %get-tuple-element.58), channel_id=1, source_target_pairs={{0,6},{1,7},{2,4},{3,5},{4,2},{5,3},{6,0},{7,1},{8,14},{9,15},{10,... | collective-permute-start | bytes 393224 | tf_op jit(solution)/shard_map/ppermute | solution.py:378
  169.9 13.8 %collective-permute-start.39 = (f32[256,128]{1,0:T(8,128)S(1)}, f32[256,128]{1,0:T(8,128)S(1)}, u32[]{:S(2)}, u32[]{:S(2)}) collective-permute-start(f32[256,128]{1,0:T(8,128)S(1)} %get-tuple-element.58), channel_id=1, source_target_pairs={{0,4},{1,5},{2,6},{3,7},{4,0},{5,1},{6,2},{7,3},{8,12},{9,13},{10,... | collective-permute-start | bytes 393224 | tf_op jit(solution)/shard_map/ppermute | solution.py:378
  172.3 13.4 %collective-permute-start.37 = (f32[256,128]{1,0:T(8,128)S(1)}, f32[256,128]{1,0:T(8,128)S(1)}, u32[]{:S(2)}, u32[]{:S(2)}) collective-permute-start(f32[256,128]{1,0:T(8,128)S(1)} %get-tuple-element.58), channel_id=1, source_target_pairs={{0,2},{1,3},{2,0},{3,1},{4,6},{5,7},{6,4},{7,5},{8,10},{9,11},{10,... | collective-permute-start | bytes 393224 | tf_op jit(solution)/shard_map/ppermute | solution.py:378
  177.9 7.7 %collective-permute-start.42 = (f32[256,128]{1,0:T(8,128)S(1)}, f32[256,128]{1,0:T(8,128)S(1)}, u32[]{:S(2)}, u32[]{:S(2)}) collective-permute-start(f32[256,128]{1,0:T(8,128)S(1)} %collective-permute-done.41.refs_6_), channel_id=1, source_target_pairs={{0,1},{1,0},{2,3},{3,2},{4,5},{5,4},{6,7},{7,6},{8,9},{9,8},{10,11... | collective-permute-start | bytes 393224 | tf_op jit(solution)/shard_map/ppermute | solution.py:378
  (25 other events, 148.0 us)
